TPU v7x, 256 devices: a whole 4x4x8 slice. The times are simulated.
256 devices in a mesh: expert: 64 (over y, z, core), dp: 4 (over x).
Axes of the slice: x: 4, y: 4, z: 8, core: 2. Of those that a mesh axis runs over, the one named last changes fastest.
Arguments:
- tokens: bfloat16 [32768, 1440], P(('expert', 'dp')), may hold values from -6 to 6
- routes: int32 [32768, 4], P(('expert', 'dp')), may hold values from 0 to 63, as said below
- gate_fixed: int32 [32768, 4], P(('expert', 'dp')), may hold values from 4096 to 65535
- counts: int32 [256], P(('expert', 'dp')), may hold values from 32 to 128, as said below
- replica_plan: int32 [8], replicated, may hold values from 0 to 63, as said below
- weight_in: bfloat16 [64, 1440, 1440], P('expert', None, 'dp'), may hold values from -0.15625 to 0.15625
- weight_out: bfloat16 [64, 1440, 1440], P('expert', 'dp'), may hold values from -0.15625 to 0.15625
- cotangent: bfloat16 [32768, 1440], P(('expert', 'dp')), may hold values from -0.59765625 to 0.59765625
Outputs:
- layer_output: bfloat16 [32768, 1440], P(('expert', 'dp'))
- input_grads: bfloat16 [32768, 1440], P(('expert', 'dp'))
- weight_in_grad: bfloat16 [64, 1440, 1440], P('expert', None, 'dp')
- weight_out_grad: bfloat16 [64, 1440, 1440], P('expert', 'dp')
Inputs may be any that keep to these rules, and one draw needn't show every extreme that they name: `routes`: each row names 4 different experts. `replica_plan`: 8 different experts, among them 0, 31, 32 and 63, in any order. `counts`: some device has 128 live tokens in every draw.
All inputs are finite; a program needn't handle non-finite values.
Results may differ from a plain program's by a relative error of at most 0.0064.
Values may be sent and summed in bfloat16 or wider, within the bound.
No kernel may reach another device: no remote copies, remote signals or barrier semaphores. Data moves between devices by JAX's collectives and lax.ppermute only.
A program may use at most 128 MiB of HBM per device.

v0:
```python
import jax
import jax.numpy as jnp
from jax import lax
from jax.experimental import pallas as pl
from jax.experimental.pallas import tpu as pltpu
from jax.sharding import PartitionSpec as P

F32 = jnp.float32
BF16 = jnp.bfloat16
VMEM_BYTES = 40 * 1024 * 1024


def moved(value, steps):
    count = lax.axis_size("dp")
    return lax.ppermute(value, "dp", [(s, (s + steps) % count) for s in range(count)])


def ring(one, two):
    left_one = moved(one, 1)
    right_two = moved(two, -1)
    left_two = moved(two, 1)
    right_one = moved(one, -1)
    far_one = moved(left_one, 1)
    far_two = moved(right_two, -1)
    return (left_one, left_two), (right_one, right_two), (far_one, far_two)


def dot(a, b, ca, cb):
    return lax.dot_general(a, b, (((ca,), (cb,)), ((), ())), preferred_element_type=F32)


def call(body, outs, flops, *args, smem=0):
    specs = [pl.BlockSpec(memory_space=pltpu.SMEM)] * smem
    specs += [pl.BlockSpec(memory_space=pltpu.VMEM)] * (len(args) - smem)
    shapes = [jax.ShapeDtypeStruct(s, d) for s, d in outs]
    moved_bytes = sum(a.size * a.dtype.itemsize for a in (*args, *shapes))
    return pl.pallas_call(
        body,
        out_shape=shapes,
        in_specs=specs,
        out_specs=[pl.BlockSpec(memory_space=pltpu.VMEM)] * len(outs),
        compiler_params=pltpu.CompilerParams(vmem_limit_bytes=VMEM_BYTES),
        cost_estimate=pl.CostEstimate(
            flops=flops, transcendentals=0, bytes_accessed=moved_bytes
        ),
    )(*args)


def prepare_body(capacity, spare):
    width = capacity + spare

    def body(count_ref, plan_ref, routes_ref, gates_ref, tok_ref, cot_ref, send_ref, get_ref):
        top_count, token_count = routes_ref.shape
        experts = send_ref.shape[0] // (2 * width)
        routes = routes_ref[...]
        gates = gates_ref[...].astype(F32)
        ids = lax.broadcasted_iota(jnp.int32, (experts, token_count), 0)
        times = lax.broadcasted_iota(jnp.int32, (experts, token_count), 1)
        hits = jnp.zeros((experts, token_count), F32)
        gate = jnp.zeros((experts, token_count), F32)
        for k in range(top_count):
            same = routes[k : k + 1, :] == ids
            hits = hits + jnp.where(same, 1.0, 0.0)
            gate = gate + jnp.where(same, gates[k : k + 1, :], 0.0)
        hits = jnp.where(times < count_ref[0], hits, 0.0)
        earlier = lax.broadcasted_iota(
            jnp.int32, (token_count, token_count), 0
        ) < lax.broadcasted_iota(jnp.int32, (token_count, token_count), 1)
        before = dot(hits.astype(BF16), jnp.where(earlier, 1.0, 0.0).astype(BF16), 1, 0)
        limit = jnp.full((experts, token_count), float(capacity), F32)
        hot = jnp.zeros((experts, token_count), F32)
        for i in range(plan_ref.shape[0]):
            hot = jnp.where(ids == plan_ref[i], 1.0, hot)
        limit = limit + float(spare) * hot
        place = jnp.where((hits > 0.0) & (before < limit), before, -1.0)
        rows = experts * 2 * width

        def spread(value):
            return jnp.broadcast_to(
                value[:, None, :], (experts, 2 * width, token_count)
            ).reshape(rows, token_count)

        row = lax.broadcasted_iota(jnp.int32, (rows, token_count), 0) % (2 * width)
        first = row < width
        slot = jnp.where(first, row, row - width).astype(F32)
        keep = spread(place) == slot
        one = jnp.where(keep, 1.0, 0.0)
        level = jnp.where(keep, spread(gate), 0.0)
        high = jnp.floor(level * (1.0 / 256.0))
        low = (level - 256.0 * high) * (1.0 / 65536.0)
        high = high * (1.0 / 256.0)
        zero = jnp.zeros_like(one)
        sending = jnp.concatenate(
            [
                jnp.where(first, one, zero).astype(BF16),
                jnp.where(first, zero, high).astype(BF16),
                jnp.where(first, zero, low).astype(BF16),
            ],
            axis=1,
        )
        source = jnp.concatenate([tok_ref[...], cot_ref[...], cot_ref[...]], axis=1)
        send_ref[...] = dot(sending, source, 1, 1).astype(BF16)
        get_ref[0:token_count, :] = jnp.where(first, high, zero).T.astype(BF16)
        get_ref[token_count : 2 * token_count, :] = jnp.where(first, low, zero).T.astype(BF16)
        get_ref[2 * token_count :, :] = jnp.where(first, zero, one).T.astype(BF16)

    return body


def place_matrix(rows, width, by_column):
    r = lax.broadcasted_iota(jnp.int32, (rows, rows), 1 if by_column else 0)
    q = lax.broadcasted_iota(jnp.int32, (rows, rows), 0 if by_column else 1)
    half = rows // 2
    second = r >= half
    inner = jnp.where(second, r - half, r)
    chunk = (inner // width) * (2 * width) + inner % width + jnp.where(second, width, 0)
    return jnp.where(q == chunk, 1.0, 0.0).astype(BF16)


def pack_body(width):
    def body(in_ref, x_ref, y_ref, xt_ref, yt_ref):
        rows = in_ref.shape[0]
        packed = dot(place_matrix(rows, width, False), in_ref[...], 1, 0).astype(BF16)
        x_ref[...] = packed[: rows // 2]
        y_ref[...] = packed[rows // 2 :]
        xt_ref[...] = packed[: rows // 2].T
        yt_ref[...] = packed[rows // 2 :].T

    return body


def hidden_terms(x, y, wi, wo):
    pre = dot(x, wi, 1, 0)
    s = jax.nn.sigmoid(1.702 * pre)
    act = (pre * s).astype(BF16)
    grad = dot(y, wo, 1, 1) * (s + 1.702 * pre * s * (1.0 - s))
    return act, grad.astype(BF16)


def near_body(x_ref, y_ref, *refs):
    out_ref, dx_ref = refs[-2:]
    weights = refs[:-2]
    x = x_ref[...]
    y = y_ref[...]
    for i in range(0, len(weights), 2):
        wi = weights[i][...]
        wo = weights[i + 1][...]
        act, grad = hidden_terms(x, y, wi, wo)
        if i == 0:
            out_ref[...] = dot(act, wo, 1, 0)
            dx_ref[...] = dot(grad, wi, 1, 1)
        else:
            out_ref[...] += dot(act, wo, 1, 0)
            dx_ref[...] += dot(grad, wi, 1, 1)


def far_body(width):
    def body(x_ref, y_ref, wi_ref, wo_ref, out_ref, dx_ref, back_ref):
        wi = wi_ref[...]
        wo = wo_ref[...]
        act, grad = hidden_terms(x_ref[...], y_ref[...], wi, wo)
        out = (out_ref[...] + dot(act, wo, 1, 0)).astype(BF16)
        dx = (dx_ref[...] + dot(grad, wi, 1, 1)).astype(BF16)
        rows = back_ref.shape[0]
        both = jnp.concatenate([out, dx], axis=0)
        back_ref[...] = dot(place_matrix(rows, width, True), both, 1, 0).astype(BF16)

    return body


def weight_terms(wi_t, wo, x, y):
    pre = dot(wi_t, x, 1, 0)
    s = jax.nn.sigmoid(1.702 * pre)
    act = (pre * s).astype(BF16)
    grad = (dot(wo, y, 1, 0) * (s + 1.702 * pre * s * (1.0 - s))).astype(BF16)
    return dot(grad, x, 1, 1), dot(act, y, 1, 1)


def near_weights_body(wi_ref, wo_ref, *refs):
    gi_ref, go_ref = refs[-2:]
    blocks = refs[:-2]
    wi_t = wi_ref[...]
    wo = wo_ref[...]
    for i in range(0, len(blocks), 2):
        term_in, term_out = weight_terms(wi_t, wo, blocks[i][...], blocks[i + 1][...])
        if i == 0:
            gi_ref[...] = term_in
            go_ref[...] = term_out
        else:
            gi_ref[...] += term_in
            go_ref[...] += term_out


def far_weights_body(wi_ref, wo_ref, x_ref, y_ref, si_ref, so_ref, gi_ref, go_ref):
    term_in, term_out = weight_terms(wi_ref[...], wo_ref[...], x_ref[...], y_ref[...])
    go_ref[...] = (so_ref[...] + term_out).astype(BF16)
    gi_ref[...] = (si_ref[...] + term_in).astype(BF16).T


def turn_body(in_ref, out_ref):
    out_ref[...] = in_ref[...].T


def finish_body(get_ref, back_ref, layer_ref, grads_ref):
    token_count = get_ref.shape[0] // 3
    final = dot(get_ref[...], back_ref[...], 1, 0)
    layer = final[:token_count] + final[token_count : 2 * token_count]
    layer_ref[...] = layer.T.astype(BF16)
    grads_ref[...] = final[2 * token_count :].T.astype(BF16)


def on_device(tokens, routes, gate_fixed, counts, replica_plan, weight_in, weight_out, cotangent):
    token_count, features = tokens.shape
    top_count = routes.shape[1]
    groups = lax.axis_size("expert")
    experts = groups * weight_in.shape[0]
    capacity = 3 * token_count * top_count // (8 * experts)
    spare = capacity // 2
    width = capacity + spare
    rows = experts * 2 * width
    half = rows // 2
    wi = weight_in[0]
    wo = weight_out[0]
    hidden = wo.shape[0]
    left_w, right_w, far_w = ring(wi, wo)
    send, get = call(
        prepare_body(capacity, spare),
        [((rows, features), BF16), ((3 * token_count, rows), BF16)],
        2 * rows * 3 * token_count * features,
        counts,
        replica_plan,
        routes.T,
        gate_fixed.T,
        tokens.T,
        cotangent.T,
        smem=2,
    )
    inbound = lax.all_to_all(
        send.reshape(experts, 2 * width, features), "expert", split_axis=0, concat_axis=0, tiled=True
    ).reshape(rows, features)
    product = 2 * half * features * hidden
    wi_late, left_w, right_w = lax.optimization_barrier((wi, left_w, right_w))
    (wi_t,) = call(turn_body, [((hidden, features), BF16)], 400 * product, wi_late)
    inbound, wi_t = lax.optimization_barrier((inbound, wi_t))
    x, y, xt, yt = call(
        pack_body(width),
        [((half, features), BF16)] * 2 + [((features, half), BF16)] * 2,
        2 * rows * rows * features,
        inbound,
    )
    out, dx = call(
        near_body,
        [((half, features), F32)] * 2,
        12 * product,
        x,
        y,
        wi,
        wo,
        *left_w,
        *right_w,
    )
    xt, yt, out = lax.optimization_barrier((xt, yt, out))
    left_r, right_r, far_r = ring(xt, yt)
    (back,) = call(
        far_body(width),
        [((rows, features), BF16)],
        4 * product + 2 * rows * rows * features,
        x,
        y,
        *far_w,
        out,
        dx,
    )
    returned = lax.all_to_all(
        back.reshape(experts, 2 * width, features), "expert", split_axis=0, concat_axis=0, tiled=True
    ).reshape(rows, features)
    sum_in, sum_out = call(
        near_weights_body,
        [((hidden, features), F32)] * 2,
        100 * product,
        wi_t,
        wo,
        xt,
        yt,
        *left_r,
        *right_r,
    )
    grad_in, grad_out = call(
        far_weights_body,
        [((features, hidden), BF16), ((hidden, features), BF16)],
        4 * product,
        wi_t,
        wo,
        *far_r,
        sum_in,
        sum_out,
    )
    layer, grads = call(
        finish_body,
        [((features, token_count), BF16)] * 2,
        2 * rows * 3 * token_count * features,
        get,
        returned,
    )
    return (layer.T, grads.T, grad_in[None], grad_out[None])


def solution(mesh):
    return jax.shard_map(
        on_device,
        mesh=mesh,
        in_specs=(
            P(("expert", "dp"), None),
            P(("expert", "dp"), None),
            P(("expert", "dp"), None),
            P(("expert", "dp")),
            P(),
            P("expert", None, "dp"),
            P("expert", "dp", None),
            P(("expert", "dp"), None),
        ),
        out_specs=(
            P(("expert", "dp"), None),
            P(("expert", "dp"), None),
            P("expert", None, "dp"),
            P("expert", "dp", None),
        ),
        check_vma=False,
    )
```

profile of v0, /device:TPU:1, one launch (start us, length us, event | category | flops | bytes accessed | tf_op | source)
XLA Modules:
  0.0 143.4 jit_solution(10305686997884361875)
XLA Ops:
  0.6 3.4 %collective-permute-start.2 = (bf16[1440,360]{1,0:T(8,128)(2,1)}, bf16[1440,360]{1,0:T(8,128)(2,1)}, u32[]{:S(2)}, u32[]{:S(2)}) collective-permute-start(bf16[1440,360]{1,0:T(8,128)(2,1)} %bitcast.21), channel_id=1, source_target_pairs={{0,3},{1,0},{2,1},{3,2},{4,7},{5,4},{6,5},{7,6},{8,11},{9,8},{10,9... | collective-permute-start | bytes 3110408 | tf_op jit(solution)/shard_map/ppermute | solution.py:15
  4.0 2.7 %collective-permute-start.3 = (bf16[360,1440]{1,0:T(8,128)(2,1)}, bf16[360,1440]{1,0:T(8,128)(2,1)}, u32[]{:S(2)}, u32[]{:S(2)}) collective-permute-start(bf16[360,1440]{1,0:T(8,128)(2,1)} %bitcast.16), channel_id=1, source_target_pairs={{0,3},{1,0},{2,1},{3,2},{4,7},{5,4},{6,5},{7,6},{8,11},{9,8},{10,9... | collective-permute-start | bytes 3110408 | tf_op jit(solution)/shard_map/ppermute | solution.py:15
  11.3 3.0 %shard_map.111 = (bf16[512,1440]{1,0:T(8,128)(2,1)}, bf16[384,512]{1,0:T(8,128)(2,1)S(1)}) custom-call(s32[1]{0:T(128)S(6)} %copy.12.count_ref, s32[8]{0:T(128)S(1)} %copy-done.10, s32[4,128]{1,0:T(4,128)S(1)} %bitcast.27, s32[4,128]{1,0:T(4,128)S(1)} %bitcast.28, bf16[1440,128]{1,0:T(8,128)(2,1)S(1)} %bitcast.25, bf16[1440,128]{1,0:T(8,128)(2,1)S(1)} %bitcast.26), custom_call_target="tpu_custom_call" | custom-call | flops 566231040 | bytes 2609188 | tf_op jit(solution)/shard_map/pallas_call | solution.py:37
  15.1 13.3 %all-to-all-start = ((bf16[64,8,1440]{2,1,0:T(8,128)(2,1)}), bf16[64,8,1440]{2,1,0:T(8,128)(2,1)S(1)}, u32[]{:S(2)}, u32[]{:S(2)}) async-start(bf16[64,8,1440]{2,1,0:T(8,128)(2,1)} %bitcast.4), calls=%async_computation | async-start | bytes 3145728 | tf_op jit(solution)/shard_map/all_to_all | solution.py:238
  28.4 2.1 %collective-permute-done.refs_2_ = bf16[1440,360]{1,0:T(8,128)(2,1)} collective-permute-done((bf16[1440,360]{1,0:T(8,128)(2,1)}, bf16[1440,360]{1,0:T(8,128)(2,1)}, u32[]{:S(2)}, u32[]{:S(2)}) %collective-permute-start) | collective-permute-done | bytes 1036832 | tf_op jit(solution)/shard_map/ppermute | solution.py:15
  30.5 20.6 %collective-permute-done.3.refs_5_ = bf16[360,1440]{1,0:T(8,128)(2,1)} collective-permute-done((bf16[360,1440]{1,0:T(8,128)(2,1)}, bf16[360,1440]{1,0:T(8,128)(2,1)}, u32[]{:S(2)}, u32[]{:S(2)}) %collective-permute-start.3) | collective-permute-done | bytes 1036832 | tf_op jit(solution)/shard_map/ppermute | solution.py:15
  51.1 3.1 %collective-permute-done.1.refs_3_ = bf16[360,1440]{1,0:T(8,128)(2,1)} collective-permute-done((bf16[360,1440]{1,0:T(8,128)(2,1)}, bf16[360,1440]{1,0:T(8,128)(2,1)}, u32[]{:S(2)}, u32[]{:S(2)}) %collective-permute-start.1) | collective-permute-done | bytes 1036832 | tf_op jit(solution)/shard_map/ppermute | solution.py:15
  54.2 2.7 %collective-permute-start.5 = (bf16[360,1440]{1,0:T(8,128)(2,1)}, bf16[360,1440]{1,0:T(8,128)(2,1)}, u32[]{:S(2)}, u32[]{:S(2)}) collective-permute-start(bf16[360,1440]{1,0:T(8,128)(2,1)} %collective-permute-done.3.refs_5_), channel_id=1, source_target_pairs={{0,3},{1,0},{2,1},{3,2},{4,7},{5,4},{6,5},{7,6},{8,11},{9,8},{10,9... | collective-permute-start | bytes 3110408 | tf_op jit(solution)/shard_map/ppermute | solution.py:15
  58.2 10.0 %all-to-all-done = bf16[64,8,1440]{2,1,0:T(8,128)(2,1)S(1)} async-done(((bf16[64,8,1440]{2,1,0:T(8,128)(2,1)}), bf16[64,8,1440]{2,1,0:T(8,128)(2,1)S(1)}, u32[]{:S(2)}, u32[]{:S(2)}) %all-to-all-start) | async-done | bytes 1474592 | tf_op jit(solution)/shard_map/all_to_all | solution.py:238
  68.2 1.9 %shard_map.113 = (bf16[256,1440]{1,0:T(8,128)(2,1)S(1)}, bf16[256,1440]{1,0:T(8,128)(2,1)S(1)}, bf16[1440,256]{1,0:T(8,128)(2,1)S(1)}, bf16[1440,256]{1,0:T(8,128)(2,1)}) custom-call(bf16[512,1440]{1,0:T(8,128)(2,1)S(1)} %bitcast.15), custom_call_target="tpu_custom_call" | custom-call | flops 754974720 | bytes 4423680 | tf_op jit(solution)/shard_map/pallas_call | solution.py:37
  70.1 7.4 %shard_map.114 = (f32[256,1440]{1,0:T(8,128)S(1)}, f32[256,1440]{1,0:T(8,128)S(1)}) custom-call(bf16[256,1440]{1,0:T(8,128)(2,1)S(1)} %get-tuple-element.32.x_ref, bf16[256,1440]{1,0:T(8,128)(2,1)S(1)} %get-tuple-element.33.y_ref, bf16[1440,360]{1,0:T(8,128)(2,1)S(1)} %bitcast.24, bf16[360,1440]{1,0:T(8,128)(2,1)S(1)} %bitcast.18, ...), custom_call_target="tpu_custom_call" | custom-call | flops 3185049600 | bytes 10644480 | tf_op jit(solution)/shard_map/pallas_call | solution.py:37
  77.7 3.0 %collective-permute-start.8 = (bf16[1440,256]{1,0:T(8,128)(2,1)}, bf16[1440,256]{1,0:T(8,128)(2,1)}, u32[]{:S(2)}, u32[]{:S(2)}) collective-permute-start(bf16[1440,256]{1,0:T(8,128)(2,1)} %get-tuple-element.47.refs_1_), channel_id=1, source_target_pairs={{0,3},{1,0},{2,1},{3,2},{4,7},{5,4},{6,5},{7,6},{8,11},{9,8},{10,9... | collective-permute-start | bytes 2211848 | tf_op jit(solution)/shard_map/ppermute | solution.py:15
  80.7 1.4 collective-permute-start.11
  82.2 5.4 %shard_map.115 = bf16[512,1440]{1,0:T(8,128)(2,1)} custom-call(bf16[256,1440]{1,0:T(8,128)(2,1)S(1)} %get-tuple-element.32.x_ref, bf16[256,1440]{1,0:T(8,128)(2,1)S(1)} %get-tuple-element.33.y_ref, bf16[1440,360]{1,0:T(8,128)(2,1)} %collective-permute-done.4.wi_ref, bf16[360,1440]{1,0:T(8,128)(2,1)} %collective-permute-done.5.wo_ref, ...), custom_call_target="tpu_custom_call" | custom-call | flops 1816657920 | bytes 7971840 | tf_op jit(solution)/shard_map/pallas_call | solution.py:37
  87.6 14.4 %all-to-all-start.1 = ((bf16[64,8,1440]{2,1,0:T(8,128)(2,1)}), bf16[64,8,1440]{2,1,0:T(8,128)(2,1)S(1)}, u32[]{:S(2)}, u32[]{:S(2)}) async-start(bf16[64,8,1440]{2,1,0:T(8,128)(2,1)} %bitcast.8), calls=%async_computation.1 | async-start | bytes 3145728 | tf_op jit(solution)/shard_map/all_to_all | solution.py:274
  102.1 3.0 %collective-permute-start.9 = (bf16[1440,256]{1,0:T(8,128)(2,1)}, bf16[1440,256]{1,0:T(8,128)(2,1)S(1)}, u32[]{:S(2)}, u32[]{:S(2)}) collective-permute-start(bf16[1440,256]{1,0:T(8,128)(2,1)} %collective-permute-done.8.refs_5_), channel_id=1, source_target_pairs={{0,3},{1,0},{2,1},{3,2},{4,7},{5,4},{6,5},{7,6},{8,11},{9,8},{10,9... | collective-permute-start | bytes 2211848 | tf_op jit(solution)/shard_map/ppermute | solution.py:15
  105.1 7.4 %collective-permute-done.11.refs_4_ = bf16[1440,256]{1,0:T(8,128)(2,1)} collective-permute-done((bf16[1440,256]{1,0:T(8,128)(2,1)S(1)}, bf16[1440,256]{1,0:T(8,128)(2,1)}, u32[]{:S(2)}, u32[]{:S(2)}) %collective-permute-start.11) | collective-permute-done | bytes 737312 | tf_op jit(solution)/shard_map/ppermute | solution.py:15
  112.5 1.1 collective-permute-done.10.refs_3_
  113.5 1.2 copy-done.2
  114.8 6.2 %shard_map.117 = (f32[360,1440]{1,0:T(8,128)S(1)}, f32[360,1440]{1,0:T(8,128)S(1)}) custom-call(bf16[360,1440]{1,0:T(8,128)(2,1)S(1)} %copy-done.2, bf16[360,1440]{1,0:T(8,128)(2,1)S(1)} %bitcast.19, bf16[1440,256]{1,0:T(8,128)(2,1)S(1)} %get-tuple-element.46.refs_0_, bf16[1440,256]{1,0:T(8,128)(2,1)} %get-tuple-element.47.refs_1_, ...), custom_call_target="tpu_custom_call" | custom-call | flops 26542080000 | bytes 10644480 | tf_op jit(solution)/shard_map/pallas_call | solution.py:37
  120.9 8.3 %collective-permute-done.7.x_ref = bf16[1440,256]{1,0:T(8,128)(2,1)S(1)} collective-permute-done((bf16[1440,256]{1,0:T(8,128)(2,1)}, bf16[1440,256]{1,0:T(8,128)(2,1)S(1)}, u32[]{:S(2)}, u32[]{:S(2)}) %collective-permute-start.7) | collective-permute-done | bytes 737312 | tf_op jit(solution)/shard_map/ppermute | solution.py:15
  129.2 2.8 %shard_map.118 = (bf16[1440,360]{1,0:T(8,128)(2,1)}, bf16[360,1440]{1,0:T(8,128)(2,1)}) custom-call(bf16[360,1440]{1,0:T(8,128)(2,1)S(1)} %copy-done.3, bf16[360,1440]{1,0:T(8,128)(2,1)S(1)} %bitcast.20, bf16[1440,256]{1,0:T(8,128)(2,1)S(1)} %collective-permute-done.7.x_ref, bf16[1440,256]{1,0:T(8,128)(2,1)S(1)} %collective-permute-done.9.y_ref, ...), custom_call_target="tpu_custom_call" | custom-call | flops 1061683200 | bytes 9768960 | tf_op jit(solution)/shard_map/pallas_call | solution.py:37
  132.1 9.7 %all-to-all-done.1 = bf16[64,8,1440]{2,1,0:T(8,128)(2,1)S(1)} async-done(((bf16[64,8,1440]{2,1,0:T(8,128)(2,1)}), bf16[64,8,1440]{2,1,0:T(8,128)(2,1)S(1)}, u32[]{:S(2)}, u32[]{:S(2)}) %all-to-all-start.1) | async-done | bytes 1474592 | tf_op jit(solution)/shard_map/all_to_all | solution.py:274
  141.8 1.7 %shard_map.116 = (bf16[1440,128]{1,0:T(8,128)(2,1)}, bf16[1440,128]{1,0:T(8,128)(2,1)}) custom-call(bf16[384,512]{1,0:T(8,128)(2,1)S(1)} %copy-done.12, bf16[512,1440]{1,0:T(8,128)(2,1)S(1)} %bitcast.14), custom_call_target="tpu_custom_call" | custom-call | flops 566231040 | bytes 2605056 | tf_op jit(solution)/shard_map/pallas_call | solution.py:37
  (38 shorter events, 6.4 us)
Async XLA Ops:
  0.6 27.8 %collective-permute-start.2 = (bf16[1440,360]{1,0:T(8,128)(2,1)}, bf16[1440,360]{1,0:T(8,128)(2,1)}, u32[]{:S(2)}, u32[]{:S(2)}) collective-permute-start(bf16[1440,360]{1,0:T(8,128)(2,1)} %bitcast.21), channel_id=1, source_target_pairs={{0,3},{1,0},{2,1},{3,2},{4,7},{5,4},{6,5},{7,6},{8,11},{9,8},{10,9... | collective-permute-start | bytes 3110408 | tf_op jit(solution)/shard_map/ppermute | solution.py:15
  4.0 26.5 %collective-permute-start = (bf16[1440,360]{1,0:T(8,128)(2,1)}, bf16[1440,360]{1,0:T(8,128)(2,1)}, u32[]{:S(2)}, u32[]{:S(2)}) collective-permute-start(bf16[1440,360]{1,0:T(8,128)(2,1)} %bitcast.22), channel_id=1, source_target_pairs={{0,1},{1,2},{2,3},{3,0},{4,5},{5,6},{6,7},{7,4},{8,9},{9,10},{10,1... | collective-permute-start | bytes 3110408 | tf_op jit(solution)/shard_map/ppermute | solution.py:15
  4.0 47.1 %collective-permute-start.3 = (bf16[360,1440]{1,0:T(8,128)(2,1)}, bf16[360,1440]{1,0:T(8,128)(2,1)}, u32[]{:S(2)}, u32[]{:S(2)}) collective-permute-start(bf16[360,1440]{1,0:T(8,128)(2,1)} %bitcast.16), channel_id=1, source_target_pairs={{0,3},{1,0},{2,1},{3,2},{4,7},{5,4},{6,5},{7,6},{8,11},{9,8},{10,9... | collective-permute-start | bytes 3110408 | tf_op jit(solution)/shard_map/ppermute | solution.py:15
  6.7 47.5 %collective-permute-start.1 = (bf16[360,1440]{1,0:T(8,128)(2,1)}, bf16[360,1440]{1,0:T(8,128)(2,1)}, u32[]{:S(2)}, u32[]{:S(2)}) collective-permute-start(bf16[360,1440]{1,0:T(8,128)(2,1)} %bitcast.17), channel_id=1, source_target_pairs={{0,1},{1,2},{2,3},{3,0},{4,5},{5,6},{6,7},{7,4},{8,9},{9,10},{10,1... | collective-permute-start | bytes 3110408 | tf_op jit(solution)/shard_map/ppermute | solution.py:15
  7.3 1.0 copy-start.6
  8.3 1.0 copy-start.7
  14.3 0.8 copy-start.11
  15.1 41.8 %copy-start.4 = (bf16[1,1440,360]{2,1,0:T(8,128)(2,1)S(1)}, bf16[1,1440,360]{2,1,0:T(8,128)(2,1)}, u32[]{:S(2)}) copy-start(bf16[1,1440,360]{2,1,0:T(8,128)(2,1)} %param.13) | copy-start | bytes 3110404
  15.1 53.1 %all-to-all-start = ((bf16[64,8,1440]{2,1,0:T(8,128)(2,1)}), bf16[64,8,1440]{2,1,0:T(8,128)(2,1)S(1)}, u32[]{:S(2)}, u32[]{:S(2)}) async-start(bf16[64,8,1440]{2,1,0:T(8,128)(2,1)} %bitcast.4), calls=%async_computation | async-start | bytes 3145728 | tf_op jit(solution)/shard_map/all_to_all | solution.py:238
  54.2 27.9 %collective-permute-start.4 = (bf16[1440,360]{1,0:T(8,128)(2,1)}, bf16[1440,360]{1,0:T(8,128)(2,1)}, u32[]{:S(2)}, u32[]{:S(2)}) collective-permute-start(bf16[1440,360]{1,0:T(8,128)(2,1)} %collective-permute-done.refs_2_), channel_id=1, source_target_pairs={{0,1},{1,2},{2,3},{3,0},{4,5},{5,6},{6,7},{7,4},{8,9},{9,10},{10,1... | collective-permute-start | bytes 3110408 | tf_op jit(solution)/shard_map/ppermute | solution.py:15
  54.2 28.0 %collective-permute-start.5 = (bf16[360,1440]{1,0:T(8,128)(2,1)}, bf16[360,1440]{1,0:T(8,128)(2,1)}, u32[]{:S(2)}, u32[]{:S(2)}) collective-permute-start(bf16[360,1440]{1,0:T(8,128)(2,1)} %collective-permute-done.3.refs_5_), channel_id=1, source_target_pairs={{0,3},{1,0},{2,1},{3,2},{4,7},{5,4},{6,5},{7,6},{8,11},{9,8},{10,9... | collective-permute-start | bytes 3110408 | tf_op jit(solution)/shard_map/ppermute | solution.py:15
  57.2 1.0 copy-start.1
  68.2 1.9 %copy-start = (bf16[1,360,1440]{2,1,0:T(8,128)(2,1)S(1)}, bf16[1,360,1440]{2,1,0:T(8,128)(2,1)}, u32[]{:S(2)}) copy-start(bf16[1,360,1440]{2,1,0:T(8,128)(2,1)} %param.14) | copy-start | bytes 3110404
  68.2 1.9 %copy-start.5 = (bf16[1,1440,360]{2,1,0:T(8,128)(2,1)S(1)}, bf16[1,1440,360]{2,1,0:T(8,128)(2,1)}, u32[]{:S(2)}) copy-start(bf16[1,1440,360]{2,1,0:T(8,128)(2,1)} %param.13) | copy-start | bytes 3110404
  77.6 24.4 %collective-permute-start.6 = (bf16[1440,256]{1,0:T(8,128)(2,1)S(1)}, bf16[1440,256]{1,0:T(8,128)(2,1)}, u32[]{:S(2)}, u32[]{:S(2)}) collective-permute-start(bf16[1440,256]{1,0:T(8,128)(2,1)S(1)} %get-tuple-element.46.refs_0_), channel_id=1, source_target_pairs={{0,1},{1,2},{2,3},{3,0},{4,5},{5,6},{6,7},{7,4},{8,9},{9,10},{10,1... | collective-permute-start | bytes 2211848 | tf_op jit(solution)/shard_map/ppermute | solution.py:15
  77.7 24.4 %collective-permute-start.8 = (bf16[1440,256]{1,0:T(8,128)(2,1)}, bf16[1440,256]{1,0:T(8,128)(2,1)}, u32[]{:S(2)}, u32[]{:S(2)}) collective-permute-start(bf16[1440,256]{1,0:T(8,128)(2,1)} %get-tuple-element.47.refs_1_), channel_id=1, source_target_pairs={{0,3},{1,0},{2,1},{3,2},{4,7},{5,4},{6,5},{7,6},{8,11},{9,8},{10,9... | collective-permute-start | bytes 2211848 | tf_op jit(solution)/shard_map/ppermute | solution.py:15
  80.7 31.8 %collective-permute-start.11 = (bf16[1440,256]{1,0:T(8,128)(2,1)S(1)}, bf16[1440,256]{1,0:T(8,128)(2,1)}, u32[]{:S(2)}, u32[]{:S(2)}) collective-permute-start(bf16[1440,256]{1,0:T(8,128)(2,1)S(1)} %get-tuple-element.46.refs_0_), channel_id=1, source_target_pairs={{0,3},{1,0},{2,1},{3,2},{4,7},{5,4},{6,5},{7,6},{8,11},{9,8},{10,9... | collective-permute-start | bytes 2211848 | tf_op jit(solution)/shard_map/ppermute | solution.py:15
  82.1 31.4 %collective-permute-start.10 = (bf16[1440,256]{1,0:T(8,128)(2,1)}, bf16[1440,256]{1,0:T(8,128)(2,1)}, u32[]{:S(2)}, u32[]{:S(2)}) collective-permute-start(bf16[1440,256]{1,0:T(8,128)(2,1)} %get-tuple-element.47.refs_1_), channel_id=1, source_target_pairs={{0,1},{1,2},{2,3},{3,0},{4,5},{5,6},{6,7},{7,4},{8,9},{9,10},{10,1... | collective-permute-start | bytes 2211848 | tf_op jit(solution)/shard_map/ppermute | solution.py:15
  87.6 54.2 %all-to-all-start.1 = ((bf16[64,8,1440]{2,1,0:T(8,128)(2,1)}), bf16[64,8,1440]{2,1,0:T(8,128)(2,1)S(1)}, u32[]{:S(2)}, u32[]{:S(2)}) async-start(bf16[64,8,1440]{2,1,0:T(8,128)(2,1)} %bitcast.8), calls=%async_computation.1 | async-start | bytes 3145728 | tf_op jit(solution)/shard_map/all_to_all | solution.py:274
  102.0 27.2 %collective-permute-start.7 = (bf16[1440,256]{1,0:T(8,128)(2,1)}, bf16[1440,256]{1,0:T(8,128)(2,1)S(1)}, u32[]{:S(2)}, u32[]{:S(2)}) collective-permute-start(bf16[1440,256]{1,0:T(8,128)(2,1)} %collective-permute-done.6.refs_2_), channel_id=1, source_target_pairs={{0,1},{1,2},{2,3},{3,0},{4,5},{5,6},{6,7},{7,4},{8,9},{9,10},{10,1... | collective-permute-start | bytes 2211848 | tf_op jit(solution)/shard_map/ppermute | solution.py:15
  102.1 27.2 %collective-permute-start.9 = (bf16[1440,256]{1,0:T(8,128)(2,1)}, bf16[1440,256]{1,0:T(8,128)(2,1)S(1)}, u32[]{:S(2)}, u32[]{:S(2)}) collective-permute-start(bf16[1440,256]{1,0:T(8,128)(2,1)} %collective-permute-done.8.refs_5_), channel_id=1, source_target_pairs={{0,3},{1,0},{2,1},{3,2},{4,7},{5,4},{6,5},{7,6},{8,11},{9,8},{10,9... | collective-permute-start | bytes 2211848 | tf_op jit(solution)/shard_map/ppermute | solution.py:15
  113.5 1.2 copy-start.2
  114.8 14.5 %copy-start.3 = (bf16[360,1440]{1,0:T(8,128)(2,1)S(1)}, bf16[360,1440]{1,0:T(8,128)(2,1)}, u32[]{:S(2)}) copy-start(bf16[360,1440]{1,0:T(8,128)(2,1)} %copy-done.1) | copy-start | bytes 3110404
  129.2 12.5 %copy-start.12 = (bf16[384,512]{1,0:T(8,128)(2,1)S(1)}, bf16[384,512]{1,0:T(8,128)(2,1)}, u32[]{:S(2)}) copy-start(bf16[384,512]{1,0:T(8,128)(2,1)} %copy-done.11) | copy-start | bytes 1179652
  (3 other events, 2.0 us)
where the time goes:
time: 144 us; the launch traced here: 143 us
  waiting for transfers between devices  62.2 us (43%)
  starting transfers between devices  44.1 us (31%)
  Pallas kernels  28.7 us (20%)
  local copies, waits for them, and re-layouts  7.01 us (5%)
    ppermute x12, waiting for transfers between devices, moved(): lax.ppermute(value, 'dp', [(s, (s + steps) % count) for s in range(count)])  42.5 us
    pallas_call x8, Pallas kernels, call(): pl.pallas_call(body, out_shape=shapes, in_specs=specs, out_specs=[pl.Bloc...  28.7 us
    ppermute x12, starting transfers between devices, moved(): lax.ppermute(value, 'dp', [(s, (s + steps) % count) for s in range(count)])  16.4 us
    all_to_all x1, starting transfers between devices, on_device(): lax.all_to_all(back.reshape(experts, 2 * width, features), 'expert', spli...  14.4 us
    all_to_all x1, starting transfers between devices, on_device(): lax.all_to_all(send.reshape(experts, 2 * width, features), 'expert', spli...  13.3 us
    all_to_all x1, waiting for transfers between devices, on_device(): lax.all_to_all(send.reshape(experts, 2 * width, features), 'expert', spli...  9.99 us
    all_to_all x1, waiting for transfers between devices, on_device(): lax.all_to_all(back.reshape(experts, 2 * width, features), 'expert', spli...  9.7 us
    unnamed x26, local copies, waits for them, and re-layouts  7.01 us
  transfers between devices with their start and end apart: 14, of which 8 were waited for; matrix products, arithmetic and copies ran while one was open for 0% of the time, Pallas kernels for 19%

commit v1 on v0

v1 whole, which is shorter than its diff:
```python
import jax
import jax.numpy as jnp
from jax import lax
from jax.experimental import pallas as pl
from jax.experimental.pallas import tpu as pltpu
from jax.sharding import PartitionSpec as P

F32 = jnp.float32
BF16 = jnp.bfloat16
VMEM_BYTES = 32 * 1024 * 1024


def moved(value, steps):
    count = lax.axis_size("dp")
    return lax.ppermute(value, "dp", [(s, (s + steps) % count) for s in range(count)])


def ring(one, two):
    left_one = moved(one, 1)
    right_two = moved(two, -1)
    left_two = moved(two, 1)
    right_one = moved(one, -1)
    far_one = moved(left_one, 1)
    far_two = moved(right_two, -1)
    return (left_one, left_two), (right_one, right_two), (far_one, far_two)


def dot(a, b, ca, cb):
    return lax.dot_general(a, b, (((ca,), (cb,)), ((), ())), preferred_element_type=F32)


def call(body, outs, flops, *args, away=(), out_away=False, scratch=()):
    kinds = [
        pl.ANY if i in away else pltpu.SMEM if a.size == 1 else pltpu.VMEM
        for i, a in enumerate(args)
    ]
    specs = [pl.BlockSpec(memory_space=kind) for kind in kinds]
    args = [
        pltpu.with_memory_space_constraint(a, pltpu.HBM) if i in away else a
        for i, a in enumerate(args)
    ]
    shapes = [jax.ShapeDtypeStruct(s, d) for s, d in outs]
    moved_bytes = sum(a.size * a.dtype.itemsize for a in (*args, *shapes))
    return pl.pallas_call(
        body,
        out_shape=shapes,
        in_specs=specs,
        out_specs=[pl.BlockSpec(memory_space=pl.ANY if out_away else pltpu.VMEM)] * len(outs),
        scratch_shapes=list(scratch),
        compiler_params=pltpu.CompilerParams(vmem_limit_bytes=VMEM_BYTES),
        cost_estimate=pl.CostEstimate(
            flops=flops, transcendentals=0, bytes_accessed=moved_bytes
        ),
    )(*args)


def fetch(pairs, sems):
    copies = [pltpu.make_async_copy(src, dst, sems.at[i]) for i, (src, dst) in enumerate(pairs)]
    for copy in copies:
        copy.start()
    return copies


def table_scratch(plan_count, top_count, token_count):
    return [
        pltpu.SMEM((plan_count,), jnp.int32),
        pltpu.VMEM((top_count, token_count), jnp.int32),
        pltpu.VMEM((top_count, token_count), jnp.int32),
    ]


def tables(count_ref, plan_ref, routes_ref, gates_ref, experts, capacity, spare):
    width = capacity + spare
    top_count, token_count = routes_ref.shape
    routes = routes_ref[...]
    gates = gates_ref[...].astype(F32)
    ids = lax.broadcasted_iota(jnp.int32, (experts, token_count), 0)
    times = lax.broadcasted_iota(jnp.int32, (experts, token_count), 1)
    hits = jnp.zeros((experts, token_count), F32)
    gate = jnp.zeros((experts, token_count), F32)
    for k in range(top_count):
        same = routes[k : k + 1, :] == ids
        hits = hits + jnp.where(same, 1.0, 0.0)
        gate = gate + jnp.where(same, gates[k : k + 1, :], 0.0)
    hits = jnp.where(times < count_ref[0], hits, 0.0)
    earlier = lax.broadcasted_iota(
        jnp.int32, (token_count, token_count), 0
    ) < lax.broadcasted_iota(jnp.int32, (token_count, token_count), 1)
    before = dot(hits.astype(BF16), jnp.where(earlier, 1.0, 0.0).astype(BF16), 1, 0)
    hot = jnp.zeros((experts, token_count), F32)
    for i in range(plan_ref.shape[0]):
        hot = jnp.where(ids == plan_ref[i], 1.0, hot)
    limit = float(capacity) + float(spare) * hot
    place = jnp.where((hits > 0.0) & (before < limit), before, -1.0)
    rows = experts * 2 * width

    def spread(value):
        return jnp.broadcast_to(
            value[:, None, :], (experts, 2 * width, token_count)
        ).reshape(rows, token_count)

    row = lax.broadcasted_iota(jnp.int32, (rows, token_count), 0) % (2 * width)
    first = row < width
    slot = jnp.where(first, row, row - width).astype(F32)
    keep = spread(place) == slot
    one = jnp.where(keep, 1.0, 0.0)
    level = jnp.where(keep, spread(gate), 0.0)
    high = jnp.floor(level * (1.0 / 256.0))
    low = (level - 256.0 * high) * (1.0 / 65536.0)
    high = high * (1.0 / 256.0)
    return first, one, high, low


def prepare_body(capacity, spare):
    def body(
        count_ref,
        plan_hbm,
        routes_hbm,
        gates_hbm,
        tok_hbm,
        cot_hbm,
        send_ref,
        plan_ref,
        routes_ref,
        gates_ref,
        source_ref,
        sems,
    ):
        token_count = routes_ref.shape[1]
        experts = send_ref.shape[0] // (2 * (capacity + spare))
        copies = fetch(
            [
                (routes_hbm, routes_ref),
                (gates_hbm, gates_ref),
                (plan_hbm, plan_ref),
                (tok_hbm, source_ref.at[:, 0:token_count]),
                (cot_hbm, source_ref.at[:, token_count : 2 * token_count]),
                (cot_hbm, source_ref.at[:, 2 * token_count : 3 * token_count]),
            ],
            sems,
        )
        for copy in copies[:3]:
            copy.wait()
        first, one, high, low = tables(
            count_ref, plan_ref, routes_ref, gates_ref, experts, capacity, spare
        )
        zero = jnp.zeros_like(one)
        sending = jnp.concatenate(
            [
                jnp.where(first, one, zero).astype(BF16),
                jnp.where(first, zero, high).astype(BF16),
                jnp.where(first, zero, low).astype(BF16),
            ],
            axis=1,
        )
        for copy in copies[3:]:
            copy.wait()
        send_ref[...] = dot(sending, source_ref[...], 1, 1).astype(BF16)

    return body


def place_matrix(rows, width, by_column):
    r = lax.broadcasted_iota(jnp.int32, (rows, rows), 1 if by_column else 0)
    q = lax.broadcasted_iota(jnp.int32, (rows, rows), 0 if by_column else 1)
    half = rows // 2
    second = r >= half
    inner = jnp.where(second, r - half, r)
    chunk = (inner // width) * (2 * width) + inner % width + jnp.where(second, width, 0)
    return jnp.where(q == chunk, 1.0, 0.0).astype(BF16)


def hidden_terms(x, y, wi, wo):
    pre = dot(x, wi, 1, 0)
    s = jax.nn.sigmoid(1.702 * pre)
    act = (pre * s).astype(BF16)
    grad = dot(y, wo, 1, 1) * (s + 1.702 * pre * s * (1.0 - s))
    return act, grad.astype(BF16)


def near_body(width):
    def body(in_ref, *refs):
        weights = refs[:6]
        x_ref, y_ref, xt_ref, yt_ref, out_ref, dx_ref, wi_buf, wo_buf, sems = refs[6:]
        copies = fetch(
            [(w, (wo_buf if i % 2 else wi_buf).at[i // 2]) for i, w in enumerate(weights)], sems
        )
        place = place_matrix(in_ref.shape[0], width, False)
        packed = dot(place, in_ref[...], 1, 0).astype(BF16)
        half = x_ref.shape[0]
        x = packed[:half]
        y = packed[half:]
        x_ref[...] = x
        y_ref[...] = y
        xt_ref[...] = x.T
        yt_ref[...] = y.T
        for i in range(3):
            copies[2 * i].wait()
            copies[2 * i + 1].wait()
            wi = wi_buf[i]
            wo = wo_buf[i]
            act, grad = hidden_terms(x, y, wi, wo)
            if i == 0:
                out_ref[...] = dot(act, wo, 1, 0)
                dx_ref[...] = dot(grad, wi, 1, 1)
            else:
                out_ref[...] += dot(act, wo, 1, 0)
                dx_ref[...] += dot(grad, wi, 1, 1)

    return body


def far_body(width):
    def body(
        x_ref, y_ref, wi_hbm, wo_hbm, out_ref, dx_ref, back_hbm, wi_buf, wo_buf, back_buf, sems, back_sems
    ):
        copies = fetch([(wi_hbm, wi_buf), (wo_hbm, wo_buf)], sems)
        rows = back_buf.shape[0]
        spread = place_matrix(rows, width, True)
        copies[0].wait()
        wi = wi_buf[...]
        pre = dot(x_ref[...], wi, 1, 0)
        s = jax.nn.sigmoid(1.702 * pre)
        act = (pre * s).astype(BF16)
        copies[1].wait()
        wo = wo_buf[...]
        grad = (dot(y_ref[...], wo, 1, 1) * (s + 1.702 * pre * s * (1.0 - s))).astype(BF16)
        out = (out_ref[...] + dot(act, wo, 1, 0)).astype(BF16)
        dx = (dx_ref[...] + dot(grad, wi, 1, 1)).astype(BF16)
        both = jnp.concatenate([out, dx], axis=0)
        step = rows // 4
        leaving = []
        for i in range(4):
            lo = i * step
            back_buf[lo : lo + step, :] = dot(spread[lo : lo + step], both, 1, 0).astype(BF16)
            copy = pltpu.make_async_copy(
                back_buf.at[pl.ds(lo, step), :], back_hbm.at[pl.ds(lo, step), :], back_sems.at[i]
            )
            copy.start()
            leaving.append(copy)
        for copy in leaving:
            copy.wait()

    return body


def weight_terms(wi_t, wo, x, y):
    pre = dot(wi_t, x, 1, 0)
    s = jax.nn.sigmoid(1.702 * pre)
    act = (pre * s).astype(BF16)
    grad = (dot(wo, y, 1, 0) * (s + 1.702 * pre * s * (1.0 - s))).astype(BF16)
    return dot(grad, x, 1, 1), dot(act, y, 1, 1)


def near_weights_body(wi_ref, wo_ref, *refs):
    gi_ref, go_ref = refs[-2:]
    blocks = refs[:-2]
    wi_t = wi_ref[...]
    wo = wo_ref[...]
    for i in range(0, len(blocks), 2):
        term_in, term_out = weight_terms(wi_t, wo, blocks[i][...], blocks[i + 1][...])
        if i == 0:
            gi_ref[...] = term_in
            go_ref[...] = term_out
        else:
            gi_ref[...] += term_in
            go_ref[...] += term_out


def far_weights_body(wi_ref, wo_ref, x_ref, y_ref, si_ref, so_ref, gi_ref, go_ref):
    term_in, term_out = weight_terms(wi_ref[...], wo_ref[...], x_ref[...], y_ref[...])
    go_ref[...] = (so_ref[...] + term_out).astype(BF16)
    gi_ref[...] = (si_ref[...] + term_in).astype(BF16).T


def idle_body(capacity, spare):
    width = capacity + spare

    def body(
        count_ref,
        plan_hbm,
        routes_hbm,
        gates_hbm,
        in_ref,
        out_ref,
        get_ref,
        plan_ref,
        routes_ref,
        gates_ref,
        sems,
    ):
        copies = fetch(
            [
                (routes_hbm, routes_ref),
                (gates_hbm, gates_ref),
                (plan_hbm, plan_ref),
            ],
            sems,
        )
        out_ref[...] = in_ref[...].T
        for copy in copies:
            copy.wait()
        token_count = routes_ref.shape[1]
        first, one, high, low = tables(
            count_ref, plan_ref, routes_ref, gates_ref, get_ref.shape[1] // (2 * width), capacity, spare
        )
        zero = jnp.zeros_like(one)
        get_ref[0:token_count, :] = jnp.where(first, high, zero).T.astype(BF16)
        get_ref[token_count : 2 * token_count, :] = jnp.where(first, low, zero).T.astype(BF16)
        get_ref[2 * token_count :, :] = jnp.where(first, zero, one).T.astype(BF16)

    return body


def finish_body(get_ref, back_ref, layer_ref, grads_ref):
    token_count = get_ref.shape[0] // 3
    final = dot(get_ref[...], back_ref[...], 1, 0)
    layer = final[:token_count] + final[token_count : 2 * token_count]
    layer_ref[...] = layer.T.astype(BF16)
    grads_ref[...] = final[2 * token_count :].T.astype(BF16)


def on_device(tokens, routes, gate_fixed, counts, replica_plan, weight_in, weight_out, cotangent):
    token_count, features = tokens.shape
    top_count = routes.shape[1]
    groups = lax.axis_size("expert")
    experts = groups * weight_in.shape[0]
    capacity = 3 * token_count * top_count // (8 * experts)
    spare = capacity // 2
    width = capacity + spare
    rows = experts * 2 * width
    half = rows // 2
    wi = weight_in[0]
    wo = weight_out[0]
    hidden = wo.shape[0]
    left_w, right_w, far_w = ring(wi, wo)
    few = (counts, replica_plan, routes.T, gate_fixed.T)
    table = table_scratch(replica_plan.shape[0], top_count, token_count)
    (send,) = call(
        prepare_body(capacity, spare),
        [((rows, features), BF16)],
        2 * rows * 3 * token_count * features,
        *few,
        tokens.T,
        cotangent.T,
        away=range(1, 6),
        scratch=[
            *table,
            pltpu.VMEM((features, 3 * token_count), BF16),
            pltpu.SemaphoreType.DMA((6,)),
        ],
    )
    inbound = lax.all_to_all(
        send.reshape(experts, 2 * width, features), "expert", split_axis=0, concat_axis=0, tiled=True
    ).reshape(rows, features)
    product = 2 * half * features * hidden
    wi_late, left_one, right_two = lax.optimization_barrier((wi, left_w[0], right_w[1]))
    wi_t, get = call(
        idle_body(capacity, spare),
        [
            ((hidden, features), BF16),
            ((3 * token_count, rows), BF16),
        ],
        100 * product,
        *few,
        wi_late,
        away=range(1, 4),
        scratch=[*table, pltpu.SemaphoreType.DMA((3,))],
    )
    inbound, wi_t = lax.optimization_barrier((inbound, wi_t))
    left_w, right_w = (left_one, left_w[1]), (right_w[0], right_two)
    x, y, xt, yt, out, dx = call(
        near_body(width),
        [((half, features), BF16)] * 2
        + [((features, half), BF16)] * 2
        + [((half, features), F32)] * 2,
        12 * product + 2 * rows * rows * features,
        inbound,
        wi,
        wo,
        *left_w,
        *right_w,
        away=range(1, 7),
        scratch=[
            pltpu.VMEM((3, features, hidden), BF16),
            pltpu.VMEM((3, hidden, features), BF16),
            pltpu.SemaphoreType.DMA((6,)),
        ],
    )
    xt, yt, out = lax.optimization_barrier((xt, yt, out))
    left_r, right_r, far_r = ring(xt, yt)
    (back,) = call(
        far_body(width),
        [((rows, features), BF16)],
        4 * product + 2 * rows * rows * features,
        x,
        y,
        *far_w,
        out,
        dx,
        away=(2, 3),
        out_away=True,
        scratch=[
            pltpu.VMEM((features, hidden), BF16),
            pltpu.VMEM((hidden, features), BF16),
            pltpu.VMEM((rows, features), BF16),
            pltpu.SemaphoreType.DMA((2,)),
            pltpu.SemaphoreType.DMA((4,)),
        ],
    )
    returned = lax.all_to_all(
        back.reshape(experts, 2 * width, features), "expert", split_axis=0, concat_axis=0, tiled=True
    ).reshape(rows, features)
    sum_in, sum_out = call(
        near_weights_body,
        [((hidden, features), F32)] * 2,
        12 * product,
        wi_t,
        wo,
        xt,
        yt,
        *left_r,
        *right_r,
    )
    grad_in, grad_out = call(
        far_weights_body,
        [((features, hidden), BF16), ((hidden, features), BF16)],
        66 * product,
        wi_t,
        wo,
        *far_r,
        sum_in,
        sum_out,
    )
    layer, grads = call(
        finish_body,
        [((features, token_count), BF16)] * 2,
        2 * rows * 3 * token_count * features,
        get,
        returned,
    )
    return (layer.T, grads.T, grad_in[None], grad_out[None])


def solution(mesh):
    return jax.shard_map(
        on_device,
        mesh=mesh,
        in_specs=(
            P(("expert", "dp"), None),
            P(("expert", "dp"), None),
            P(("expert", "dp"), None),
            P(("expert", "dp")),
            P(),
            P("expert", None, "dp"),
            P("expert", "dp", None),
            P(("expert", "dp"), None),
        ),
        out_specs=(
            P(("expert", "dp"), None),
            P(("expert", "dp"), None),
            P("expert", None, "dp"),
            P("expert", "dp", None),
        ),
        check_vma=False,
    )
```

time: 144 us -> 137 us (0.951)
  local copies, waits for them, and re-layouts: 7.01 us -> 2.99 us
  waiting for transfers between devices: 62.2 us -> 58.8 us
  starting transfers between devices: 44.1 us -> 46 us
    all_to_all x1, waiting for transfers between devices: 9.99 us -> 27.9 us  [on_device(): lax.all_to_all(send.reshape(experts, 2 * width, features), 'expert', spli...]
    ppermute x12, waiting for transfers between devices: 42.5 us -> 29 us  [moved(): lax.ppermute(value, 'dp', [(s, (s + steps) % count) for s in range(count)])]
    all_to_all x1, waiting for transfers between devices: 9.7 us -> 1.86 us  [on_device(): lax.all_to_all(back.reshape(experts, 2 * width, features), 'expert', spli...]
    unnamed x26 -> x12, local copies, waits for them, and re-layouts: 7.01 us -> 2.99 us
    pallas_call x8 -> x7, Pallas kernels: 28.7 us -> 27.8 us  [call(): pl.pallas_call(body, out_shape=shapes, in_specs=specs, out_specs=[pl.Bloc...]
where the time goes in v1:
time: 137 us
  waiting for transfers between devices  58.8 us (43%)
  starting transfers between devices  46 us (34%)
  Pallas kernels  27.8 us (20%)
  local copies, waits for them, and re-layouts  2.99 us (2%)
  between operations  1.41 us (1%)
    ppermute x12, waiting for transfers between devices, moved(): lax.ppermute(value, 'dp', [(s, (s + steps) % count) for s in range(count)])  29 us
    all_to_all x1, waiting for transfers between devices, on_device(): lax.all_to_all(send.reshape(experts, 2 * width, features), 'expert', spli...  27.9 us
    pallas_call x7, Pallas kernels, call(): pl.pallas_call(body, out_shape=shapes, in_specs=specs, out_specs=[pl.Bloc...  27.8 us
    ppermute x12, starting transfers between devices, moved(): lax.ppermute(value, 'dp', [(s, (s + steps) % count) for s in range(count)])  17.4 us
    all_to_all x1, starting transfers between devices, on_device(): lax.all_to_all(back.reshape(experts, 2 * width, features), 'expert', spli...  15.5 us
    all_to_all x1, starting transfers between devices, on_device(): lax.all_to_all(send.reshape(experts, 2 * width, features), 'expert', spli...  13.1 us
    unnamed x12, local copies, waits for them, and re-layouts  2.99 us
  transfers between devices with their start and end apart: 14, of which 8 were waited for; matrix products, arithmetic and copies ran while one was open for 0% of the time, Pallas kernels for 19%

profile of v1, /device:TPU:1, one launch (start us, length us, event | category | flops | bytes accessed | tf_op | source)
XLA Modules:
  0.0 137.0 jit_solution(3310904777191161287)
XLA Ops:
  0.6 2.1 %collective-permute-start = (bf16[1440,360]{1,0:T(8,128)(2,1)}, bf16[1440,360]{1,0:T(8,128)(2,1)}, u32[]{:S(2)}, u32[]{:S(2)}) collective-permute-start(bf16[1440,360]{1,0:T(8,128)(2,1)} %bitcast.16), channel_id=1, source_target_pairs={{0,1},{1,2},{2,3},{3,0},{4,5},{5,6},{6,7},{7,4},{8,9},{9,10},{10,1... | collective-permute-start | bytes 3110408 | tf_op jit(solution)/shard_map/ppermute | solution.py:15
  2.7 1.4 collective-permute-start.1
  4.8 3.6 %shard_map.112 = bf16[512,1440]{1,0:T(8,128)(2,1)} custom-call(s32[1]{0:T(128)S(6)} %copy.12.count_ref, s32[8]{0:T(128)} %plan_hbm.3, s32[4,128]{1,0:T(4,128)} %bitcast.27, s32[4,128]{1,0:T(4,128)} %bitcast.29, bf16[1440,128]{1,0:T(8,128)(2,1)} %bitcast.25, bf16[1440,128]{1,0:T(8,128)(2,1)} %bitcast.26), custom_call_target="tpu_custom_call" | custom-call | flops 566231040 | bytes 2215972 | tf_op jit(solution)/shard_map/pallas_call | solution.py:44
  8.3 13.1 %all-to-all-start = ((bf16[64,8,1440]{2,1,0:T(8,128)(2,1)}), bf16[64,8,1440]{2,1,0:T(8,128)(2,1)S(1)}, u32[]{:S(2)}, u32[]{:S(2)}) async-start(bf16[64,8,1440]{2,1,0:T(8,128)(2,1)} %bitcast.6), calls=%async_computation | async-start | bytes 3145728 | tf_op jit(solution)/shard_map/all_to_all | solution.py:353
  21.6 2.7 %collective-permute-start.3 = (bf16[1440,360]{1,0:T(8,128)(2,1)S(1)}, bf16[1440,360]{1,0:T(8,128)(2,1)}, u32[]{:S(2)}, u32[]{:S(2)}) collective-permute-start(bf16[1440,360]{1,0:T(8,128)(2,1)S(1)} %bitcast.18), channel_id=1, source_target_pairs={{0,3},{1,0},{2,1},{3,2},{4,7},{5,4},{6,5},{7,6},{8,11},{9,8},{10,9... | collective-permute-start | bytes 3110408 | tf_op jit(solution)/shard_map/ppermute | solution.py:15
  24.2 1.9 %collective-permute-done.refs_2_ = bf16[1440,360]{1,0:T(8,128)(2,1)} collective-permute-done((bf16[1440,360]{1,0:T(8,128)(2,1)}, bf16[1440,360]{1,0:T(8,128)(2,1)}, u32[]{:S(2)}, u32[]{:S(2)}) %collective-permute-start) | collective-permute-done | bytes 1036832 | tf_op jit(solution)/shard_map/ppermute | solution.py:15
  26.2 1.5 %collective-permute-done.1.refs_5_ = bf16[360,1440]{1,0:T(8,128)(2,1)} collective-permute-done((bf16[360,1440]{1,0:T(8,128)(2,1)}, bf16[360,1440]{1,0:T(8,128)(2,1)}, u32[]{:S(2)}, u32[]{:S(2)}) %collective-permute-start.1) | collective-permute-done | bytes 1036832 | tf_op jit(solution)/shard_map/ppermute | solution.py:15
  27.7 1.6 %collective-permute-start.4 = (bf16[1440,360]{1,0:T(8,128)(2,1)}, bf16[1440,360]{1,0:T(8,128)(2,1)}, u32[]{:S(2)}, u32[]{:S(2)}) collective-permute-start(bf16[1440,360]{1,0:T(8,128)(2,1)} %collective-permute-done.refs_2_), channel_id=1, source_target_pairs={{0,1},{1,2},{2,3},{3,0},{4,5},{5,6},{6,7},{7,4},{8,9},{9,10},{10,1... | collective-permute-start | bytes 3110408 | tf_op jit(solution)/shard_map/ppermute | solution.py:15
  33.3 27.9 %all-to-all-done = bf16[64,8,1440]{2,1,0:T(8,128)(2,1)S(1)} async-done(((bf16[64,8,1440]{2,1,0:T(8,128)(2,1)}), bf16[64,8,1440]{2,1,0:T(8,128)(2,1)S(1)}, u32[]{:S(2)}, u32[]{:S(2)}) %all-to-all-start) | async-done | bytes 1474592 | tf_op jit(solution)/shard_map/all_to_all | solution.py:353
  61.3 7.9 %shard_map.113 = (bf16[256,1440]{1,0:T(8,128)(2,1)S(1)}, bf16[256,1440]{1,0:T(8,128)(2,1)S(1)}, bf16[1440,256]{1,0:T(8,128)(2,1)S(1)}, bf16[1440,256]{1,0:T(8,12...) custom-call(bf16[512,1440]{1,0:T(8,128)(2,1)S(1)} %bitcast.15, bf16[1440,360]{1,0:T(8,128)(2,1)} %bitcast.17, ...), custom_call_target="tpu_custom_call" | custom-call | flops 3940024320 | bytes 13593600 | tf_op jit(solution)/shard_map/pallas_call | solution.py:44
  69.3 2.7 %collective-permute-start.8 = (bf16[1440,256]{1,0:T(8,128)(2,1)}, bf16[1440,256]{1,0:T(8,128)(2,1)}, u32[]{:S(2)}, u32[]{:S(2)}) collective-permute-start(bf16[1440,256]{1,0:T(8,128)(2,1)} %get-tuple-element.43.refs_1_), channel_id=1, source_target_pairs={{0,3},{1,0},{2,1},{3,2},{4,7},{5,4},{6,5},{7,6},{8,11},{9,8},{10,9... | collective-permute-start | bytes 2211848 | tf_op jit(solution)/shard_map/ppermute | solution.py:15
  72.0 1.6 %collective-permute-done.4.wi_hbm = bf16[1440,360]{1,0:T(8,128)(2,1)} collective-permute-done((bf16[1440,360]{1,0:T(8,128)(2,1)}, bf16[1440,360]{1,0:T(8,128)(2,1)}, u32[]{:S(2)}, u32[]{:S(2)}) %collective-permute-start.4) | collective-permute-done | bytes 1036832 | tf_op jit(solution)/shard_map/ppermute | solution.py:15
  73.6 1.5 %collective-permute-done.5.wo_hbm = bf16[360,1440]{1,0:T(8,128)(2,1)} collective-permute-done((bf16[360,1440]{1,0:T(8,128)(2,1)}, bf16[360,1440]{1,0:T(8,128)(2,1)}, u32[]{:S(2)}, u32[]{:S(2)}) %collective-permute-start.5) | collective-permute-done | bytes 1036832 | tf_op jit(solution)/shard_map/ppermute | solution.py:15
  75.1 4.9 %shard_map.114 = bf16[512,1440]{1,0:T(8,128)(2,1)} custom-call(bf16[256,1440]{1,0:T(8,128)(2,1)S(1)} %get-tuple-element.32.x_ref, bf16[256,1440]{1,0:T(8,128)(2,1)S(1)} %get-tuple-element.33.y_ref, bf16[1440,360]{1,0:T(8,128)(2,1)} %collective-permute-done.4.wi_hbm, bf16[360,1440]{1,0:T(8,128)(2,1)} %collective-permute-done.5.wo_hbm, ...), custom_call_target="tpu_custom_call" | custom-call | flops 1816657920 | bytes 7971840 | tf_op jit(solution)/shard_map/pallas_call | solution.py:44
  80.0 15.5 %all-to-all-start.1 = ((bf16[64,8,1440]{2,1,0:T(8,128)(2,1)}), bf16[64,8,1440]{2,1,0:T(8,128)(2,1)S(1)}, u32[]{:S(2)}, u32[]{:S(2)}) async-start(bf16[64,8,1440]{2,1,0:T(8,128)(2,1)} %bitcast.8), calls=%async_computation.1 | async-start | bytes 3145728 | tf_op jit(solution)/shard_map/all_to_all | solution.py:411
  95.5 1.5 %collective-permute-start.10 = (bf16[1440,256]{1,0:T(8,128)(2,1)}, bf16[1440,256]{1,0:T(8,128)(2,1)S(1)}, u32[]{:S(2)}, u32[]{:S(2)}) collective-permute-start(bf16[1440,256]{1,0:T(8,128)(2,1)} %get-tuple-element.43.refs_1_), channel_id=1, source_target_pairs={{0,1},{1,2},{2,3},{3,0},{4,5},{5,6},{6,7},{7,4},{8,9},{9,10},{10,1... | collective-permute-start | bytes 2211848 | tf_op jit(solution)/shard_map/ppermute | solution.py:15
  97.0 1.6 %collective-permute-start.11 = (bf16[1440,256]{1,0:T(8,128)(2,1)S(1)}, bf16[1440,256]{1,0:T(8,128)(2,1)S(1)}, u32[]{:S(2)}, u32[]{:S(2)}) collective-permute-start(bf16[1440,256]{1,0:T(8,128)(2,1)S(1)} %get-tuple-element.42.refs_0_), channel_id=1, source_target_pairs={{0,3},{1,0},{2,1},{3,2},{4,7},{5,4},{6,5},{7,6},{8,11},{9,8},{10,9... | collective-permute-start | bytes 2211848 | tf_op jit(solution)/shard_map/ppermute | solution.py:15
  98.6 2.7 %collective-permute-start.9 = (bf16[1440,256]{1,0:T(8,128)(2,1)}, bf16[1440,256]{1,0:T(8,128)(2,1)S(1)}, u32[]{:S(2)}, u32[]{:S(2)}) collective-permute-start(bf16[1440,256]{1,0:T(8,128)(2,1)} %collective-permute-done.8.refs_5_), channel_id=1, source_target_pairs={{0,3},{1,0},{2,1},{3,2},{4,7},{5,4},{6,5},{7,6},{8,11},{9,8},{10,9... | collective-permute-start | bytes 2211848 | tf_op jit(solution)/shard_map/ppermute | solution.py:15
  101.2 13.6 %collective-permute-done.10.refs_3_ = bf16[1440,256]{1,0:T(8,128)(2,1)S(1)} collective-permute-done((bf16[1440,256]{1,0:T(8,128)(2,1)}, bf16[1440,256]{1,0:T(8,128)(2,1)S(1)}, u32[]{:S(2)}, u32[]{:S(2)}) %collective-permute-start.10) | collective-permute-done | bytes 737312 | tf_op jit(solution)/shard_map/ppermute | solution.py:15
  116.1 5.7 %shard_map.116 = (f32[360,1440]{1,0:T(8,128)S(1)}, f32[360,1440]{1,0:T(8,128)S(1)}) custom-call(bf16[360,1440]{1,0:T(8,128)(2,1)S(1)} %copy-done.5, bf16[360,1440]{1,0:T(8,128)(2,1)S(1)} %bitcast.23, bf16[1440,256]{1,0:T(8,128)(2,1)S(1)} %get-tuple-element.42.refs_0_, bf16[1440,256]{1,0:T(8,128)(2,1)} %get-tuple-element.43.refs_1_, ...), custom_call_target="tpu_custom_call" | custom-call | flops 3185049600 | bytes 10644480 | tf_op jit(solution)/shard_map/pallas_call | solution.py:44
  121.8 8.9 %collective-permute-done.7.x_ref = bf16[1440,256]{1,0:T(8,128)(2,1)S(1)} collective-permute-done((bf16[1440,256]{1,0:T(8,128)(2,1)}, bf16[1440,256]{1,0:T(8,128)(2,1)S(1)}, u32[]{:S(2)}, u32[]{:S(2)}) %collective-permute-start.7) | collective-permute-done | bytes 737312 | tf_op jit(solution)/shard_map/ppermute | solution.py:15
  130.6 2.8 %shard_map.117 = (bf16[1440,360]{1,0:T(8,128)(2,1)}, bf16[360,1440]{1,0:T(8,128)(2,1)}) custom-call(bf16[360,1440]{1,0:T(8,128)(2,1)S(1)} %copy-done.5, bf16[360,1440]{1,0:T(8,128)(2,1)S(1)} %bitcast.24, bf16[1440,256]{1,0:T(8,128)(2,1)S(1)} %collective-permute-done.7.x_ref, bf16[1440,256]{1,0:T(8,128)(2,1)S(1)} %collective-permute-done.9.y_ref, ...), custom_call_target="tpu_custom_call" | custom-call | flops 17517772800 | bytes 9768960 | tf_op jit(solution)/shard_map/pallas_call | solution.py:44
  133.4 1.9 %all-to-all-done.1 = bf16[64,8,1440]{2,1,0:T(8,128)(2,1)S(1)} async-done(((bf16[64,8,1440]{2,1,0:T(8,128)(2,1)}), bf16[64,8,1440]{2,1,0:T(8,128)(2,1)S(1)}, u32[]{:S(2)}, u32[]{:S(2)}) %all-to-all-start.1) | async-done | bytes 1474592 | tf_op jit(solution)/shard_map/all_to_all | solution.py:411
  135.3 1.7 %shard_map.115 = (bf16[1440,128]{1,0:T(8,128)(2,1)}, bf16[1440,128]{1,0:T(8,128)(2,1)}) custom-call(bf16[384,512]{1,0:T(8,128)(2,1)S(1)} %copy-done.3, bf16[512,1440]{1,0:T(8,128)(2,1)S(1)} %bitcast.14), custom_call_target="tpu_custom_call" | custom-call | flops 566231040 | bytes 2605056 | tf_op jit(solution)/shard_map/pallas_call | solution.py:44
  (23 shorter events, 5.6 us)
Async XLA Ops:
  0.6 25.5 %collective-permute-start = (bf16[1440,360]{1,0:T(8,128)(2,1)}, bf16[1440,360]{1,0:T(8,128)(2,1)}, u32[]{:S(2)}, u32[]{:S(2)}) collective-permute-start(bf16[1440,360]{1,0:T(8,128)(2,1)} %bitcast.16), channel_id=1, source_target_pairs={{0,1},{1,2},{2,3},{3,0},{4,5},{5,6},{6,7},{7,4},{8,9},{9,10},{10,1... | collective-permute-start | bytes 3110408 | tf_op jit(solution)/shard_map/ppermute | solution.py:15
  2.7 24.9 %collective-permute-start.1 = (bf16[360,1440]{1,0:T(8,128)(2,1)}, bf16[360,1440]{1,0:T(8,128)(2,1)}, u32[]{:S(2)}, u32[]{:S(2)}) collective-permute-start(bf16[360,1440]{1,0:T(8,128)(2,1)} %bitcast.20), channel_id=1, source_target_pairs={{0,3},{1,0},{2,1},{3,2},{4,7},{5,4},{6,5},{7,6},{8,11},{9,8},{10,9... | collective-permute-start | bytes 3110408 | tf_op jit(solution)/shard_map/ppermute | solution.py:15
  8.3 13.2 %copy-start = (bf16[1,1440,360]{2,1,0:T(8,128)(2,1)S(1)}, bf16[1,1440,360]{2,1,0:T(8,128)(2,1)}, u32[]{:S(2)}) copy-start(bf16[1,1440,360]{2,1,0:T(8,128)(2,1)} %param.13) | copy-start | bytes 3110404
  8.3 52.9 %all-to-all-start = ((bf16[64,8,1440]{2,1,0:T(8,128)(2,1)}), bf16[64,8,1440]{2,1,0:T(8,128)(2,1)S(1)}, u32[]{:S(2)}, u32[]{:S(2)}) async-start(bf16[64,8,1440]{2,1,0:T(8,128)(2,1)} %bitcast.6), calls=%async_computation | async-start | bytes 3145728 | tf_op jit(solution)/shard_map/all_to_all | solution.py:353
  21.5 39.8 %collective-permute-start.2 = (bf16[360,1440]{1,0:T(8,128)(2,1)}, bf16[360,1440]{1,0:T(8,128)(2,1)}, u32[]{:S(2)}, u32[]{:S(2)}) collective-permute-start(bf16[360,1440]{1,0:T(8,128)(2,1)} %bitcast.21), channel_id=1, source_target_pairs={{0,1},{1,2},{2,3},{3,0},{4,5},{5,6},{6,7},{7,4},{8,9},{9,10},{10,1... | collective-permute-start | bytes 3110408 | tf_op jit(solution)/shard_map/ppermute | solution.py:15
  21.6 39.7 %collective-permute-start.3 = (bf16[1440,360]{1,0:T(8,128)(2,1)S(1)}, bf16[1440,360]{1,0:T(8,128)(2,1)}, u32[]{:S(2)}, u32[]{:S(2)}) collective-permute-start(bf16[1440,360]{1,0:T(8,128)(2,1)S(1)} %bitcast.18), channel_id=1, source_target_pairs={{0,3},{1,0},{2,1},{3,2},{4,7},{5,4},{6,5},{7,6},{8,11},{9,8},{10,9... | collective-permute-start | bytes 3110408 | tf_op jit(solution)/shard_map/ppermute | solution.py:15
  27.7 45.9 %collective-permute-start.4 = (bf16[1440,360]{1,0:T(8,128)(2,1)}, bf16[1440,360]{1,0:T(8,128)(2,1)}, u32[]{:S(2)}, u32[]{:S(2)}) collective-permute-start(bf16[1440,360]{1,0:T(8,128)(2,1)} %collective-permute-done.refs_2_), channel_id=1, source_target_pairs={{0,1},{1,2},{2,3},{3,0},{4,5},{5,6},{6,7},{7,4},{8,9},{9,10},{10,1... | collective-permute-start | bytes 3110408 | tf_op jit(solution)/shard_map/ppermute | solution.py:15
  29.2 45.8 %collective-permute-start.5 = (bf16[360,1440]{1,0:T(8,128)(2,1)}, bf16[360,1440]{1,0:T(8,128)(2,1)}, u32[]{:S(2)}, u32[]{:S(2)}) collective-permute-start(bf16[360,1440]{1,0:T(8,128)(2,1)} %collective-permute-done.1.refs_5_), channel_id=1, source_target_pairs={{0,3},{1,0},{2,1},{3,2},{4,7},{5,4},{6,5},{7,6},{8,11},{9,8},{10,9... | collective-permute-start | bytes 3110408 | tf_op jit(solution)/shard_map/ppermute | solution.py:15
  31.6 0.7 copy-start.2
  32.4 1.0 copy-start.4
  69.2 29.3 %collective-permute-start.6 = (bf16[1440,256]{1,0:T(8,128)(2,1)S(1)}, bf16[1440,256]{1,0:T(8,128)(2,1)}, u32[]{:S(2)}, u32[]{:S(2)}) collective-permute-start(bf16[1440,256]{1,0:T(8,128)(2,1)S(1)} %get-tuple-element.42.refs_0_), channel_id=1, source_target_pairs={{0,1},{1,2},{2,3},{3,0},{4,5},{5,6},{6,7},{7,4},{8,9},{9,10},{10,1... | collective-permute-start | bytes 2211848 | tf_op jit(solution)/shard_map/ppermute | solution.py:15
  69.3 29.3 %collective-permute-start.8 = (bf16[1440,256]{1,0:T(8,128)(2,1)}, bf16[1440,256]{1,0:T(8,128)(2,1)}, u32[]{:S(2)}, u32[]{:S(2)}) collective-permute-start(bf16[1440,256]{1,0:T(8,128)(2,1)} %get-tuple-element.43.refs_1_), channel_id=1, source_target_pairs={{0,3},{1,0},{2,1},{3,2},{4,7},{5,4},{6,5},{7,6},{8,11},{9,8},{10,9... | collective-permute-start | bytes 2211848 | tf_op jit(solution)/shard_map/ppermute | solution.py:15
  80.0 34.8 %copy-start.1 = (bf16[1,360,1440]{2,1,0:T(8,128)(2,1)S(1)}, bf16[1,360,1440]{2,1,0:T(8,128)(2,1)}, u32[]{:S(2)}) copy-start(bf16[1,360,1440]{2,1,0:T(8,128)(2,1)} %param.14) | copy-start | bytes 3110404
  80.0 55.3 %all-to-all-start.1 = ((bf16[64,8,1440]{2,1,0:T(8,128)(2,1)}), bf16[64,8,1440]{2,1,0:T(8,128)(2,1)S(1)}, u32[]{:S(2)}, u32[]{:S(2)}) async-start(bf16[64,8,1440]{2,1,0:T(8,128)(2,1)} %bitcast.8), calls=%async_computation.1 | async-start | bytes 3145728 | tf_op jit(solution)/shard_map/all_to_all | solution.py:411
  95.5 19.3 %collective-permute-start.10 = (bf16[1440,256]{1,0:T(8,128)(2,1)}, bf16[1440,256]{1,0:T(8,128)(2,1)S(1)}, u32[]{:S(2)}, u32[]{:S(2)}) collective-permute-start(bf16[1440,256]{1,0:T(8,128)(2,1)} %get-tuple-element.43.refs_1_), channel_id=1, source_target_pairs={{0,1},{1,2},{2,3},{3,0},{4,5},{5,6},{6,7},{7,4},{8,9},{9,10},{10,1... | collective-permute-start | bytes 2211848 | tf_op jit(solution)/shard_map/ppermute | solution.py:15
  97.0 17.8 %collective-permute-start.11 = (bf16[1440,256]{1,0:T(8,128)(2,1)S(1)}, bf16[1440,256]{1,0:T(8,128)(2,1)S(1)}, u32[]{:S(2)}, u32[]{:S(2)}) collective-permute-start(bf16[1440,256]{1,0:T(8,128)(2,1)S(1)} %get-tuple-element.42.refs_0_), channel_id=1, source_target_pairs={{0,3},{1,0},{2,1},{3,2},{4,7},{5,4},{6,5},{7,6},{8,11},{9,8},{10,9... | collective-permute-start | bytes 2211848 | tf_op jit(solution)/shard_map/ppermute | solution.py:15
  98.5 32.1 %collective-permute-start.7 = (bf16[1440,256]{1,0:T(8,128)(2,1)}, bf16[1440,256]{1,0:T(8,128)(2,1)S(1)}, u32[]{:S(2)}, u32[]{:S(2)}) collective-permute-start(bf16[1440,256]{1,0:T(8,128)(2,1)} %collective-permute-done.6.refs_2_), channel_id=1, source_target_pairs={{0,1},{1,2},{2,3},{3,0},{4,5},{5,6},{6,7},{7,4},{8,9},{9,10},{10,1... | collective-permute-start | bytes 2211848 | tf_op jit(solution)/shard_map/ppermute | solution.py:15
  98.6 32.1 %collective-permute-start.9 = (bf16[1440,256]{1,0:T(8,128)(2,1)}, bf16[1440,256]{1,0:T(8,128)(2,1)S(1)}, u32[]{:S(2)}, u32[]{:S(2)}) collective-permute-start(bf16[1440,256]{1,0:T(8,128)(2,1)} %collective-permute-done.8.refs_5_), channel_id=1, source_target_pairs={{0,3},{1,0},{2,1},{3,2},{4,7},{5,4},{6,5},{7,6},{8,11},{9,8},{10,9... | collective-permute-start | bytes 2211848 | tf_op jit(solution)/shard_map/ppermute | solution.py:15
  114.8 1.2 copy-start.5
  130.6 4.7 %copy-start.3 = (bf16[384,512]{1,0:T(8,128)(2,1)S(1)}, bf16[384,512]{1,0:T(8,128)(2,1)}, u32[]{:S(2)}) copy-start(bf16[384,512]{1,0:T(8,128)(2,1)} %copy-done.2) | copy-start | bytes 1179652

commit v2 on v1

--- a/solution.py
+++ b/solution.py
@@ -181,7 +181,7 @@
 def near_body(width):
     def body(in_ref, *refs):
         weights = refs[:6]
-        x_ref, y_ref, xt_ref, yt_ref, out_ref, dx_ref, wi_buf, wo_buf, sems = refs[6:]
+        x_ref, y_ref, out_ref, dx_ref, wi_buf, wo_buf, sems = refs[6:]
         copies = fetch(
             [(w, (wo_buf if i % 2 else wi_buf).at[i // 2]) for i, w in enumerate(weights)], sems
         )
@@ -192,8 +192,6 @@
         y = packed[half:]
         x_ref[...] = x
         y_ref[...] = y
-        xt_ref[...] = x.T
-        yt_ref[...] = y.T
         for i in range(3):
             copies[2 * i].wait()
             copies[2 * i + 1].wait()
@@ -252,13 +250,19 @@
     return dot(grad, x, 1, 1), dot(act, y, 1, 1)
 
 
+def turn_body(x_ref, y_ref, both_ref):
+    half = x_ref.shape[0]
+    both_ref[:, :half] = x_ref[...].T
+    both_ref[:, half:] = y_ref[...].T
+
+
 def near_weights_body(wi_ref, wo_ref, *refs):
     gi_ref, go_ref = refs[-2:]
-    blocks = refs[:-2]
     wi_t = wi_ref[...]
     wo = wo_ref[...]
-    for i in range(0, len(blocks), 2):
-        term_in, term_out = weight_terms(wi_t, wo, blocks[i][...], blocks[i + 1][...])
+    for i, both_ref in enumerate(refs[:-2]):
+        half = both_ref.shape[1] // 2
+        term_in, term_out = weight_terms(wi_t, wo, both_ref[:, :half], both_ref[:, half:])
         if i == 0:
             gi_ref[...] = term_in
             go_ref[...] = term_out
@@ -369,10 +373,9 @@
     )
     inbound, wi_t = lax.optimization_barrier((inbound, wi_t))
     left_w, right_w = (left_one, left_w[1]), (right_w[0], right_two)
-    x, y, xt, yt, out, dx = call(
+    x, y, out, dx = call(
         near_body(width),
         [((half, features), BF16)] * 2
-        + [((features, half), BF16)] * 2
         + [((half, features), F32)] * 2,
         12 * product + 2 * rows * rows * features,
         inbound,
@@ -387,8 +390,10 @@
             pltpu.SemaphoreType.DMA((6,)),
         ],
     )
-    xt, yt, out = lax.optimization_barrier((xt, yt, out))
-    left_r, right_r, far_r = ring(xt, yt)
+    (both,) = call(turn_body, [((features, rows), BF16)], 0, x, y)
+    left_r = moved(both, 1)
+    right_r = moved(both, -1)
+    far_r = (moved(left_r[:, :half], 1), moved(right_r[:, half:], -1))
     (back,) = call(
         far_body(width),
         [((rows, features), BF16)],
@@ -414,18 +419,17 @@
     sum_in, sum_out = call(
         near_weights_body,
         [((hidden, features), F32)] * 2,
-        12 * product,
+        8 * product,
         wi_t,
         wo,
-        xt,
-        yt,
-        *left_r,
-        *right_r,
+        both,
+        left_r,
+        right_r,
     )
     grad_in, grad_out = call(
         far_weights_body,
         [((features, hidden), BF16), ((hidden, features), BF16)],
-        66 * product,
+        50 * product,
         wi_t,
         wo,
         *far_r,

time: 137 us -> 137 us (level)
  starting transfers between devices: 46 us -> 43.9 us
  waiting for transfers between devices: 58.8 us -> 60.5 us
    all_to_all x1, waiting for transfers between devices: 1.86 us -> 6.63 us  [on_device(): lax.all_to_all(back.reshape(experts, 2 * width, features), 'expert', spli...]
    ppermute x12 -> x10, waiting for transfers between devices: 29 us -> 25.2 us  [moved(): lax.ppermute(value, 'dp', [(s, (s + steps) % count) for s in range(count)])]
    slice x0 -> x2, local copies, waits for them, and re-layouts: none -> 2.33 us  [on_device(): far_r = (moved(left_r[:, :half], 1), moved(right_r[:, half:], -1))]
    unnamed x12 -> x8, local copies, waits for them, and re-layouts: 2.99 us -> 1 us
    ppermute x12 -> x10, starting transfers between devices: 17.4 us -> 15.5 us  [moved(): lax.ppermute(value, 'dp', [(s, (s + steps) % count) for s in range(count)])]
    pallas_call x7 -> x8, Pallas kernels: 27.8 us -> 27.6 us  [call(): pl.pallas_call(body, out_shape=shapes, in_specs=specs, out_specs=[pl.Bloc...]
  transfers between devices with their start and end apart: 14 -> 12, of which waited for: 8 -> 9; matrix products, arithmetic and copies ran while one was open for 0% -> 2% of each run, Pallas kernels for 19% -> 19%
where the time goes in v2:
time: 137 us
  waiting for transfers between devices  60.5 us (44%)
  starting transfers between devices  43.9 us (32%)
  Pallas kernels  27.6 us (20%)
  local copies, waits for them, and re-layouts  3.33 us (2%)
  between operations  1.42 us (1%)
    all_to_all x1, waiting for transfers between devices, on_device(): lax.all_to_all(send.reshape(experts, 2 * width, features), 'expert', spli...  28.6 us
    pallas_call x8, Pallas kernels, call(): pl.pallas_call(body, out_shape=shapes, in_specs=specs, out_specs=[pl.Bloc...  27.6 us
    ppermute x10, waiting for transfers between devices, moved(): lax.ppermute(value, 'dp', [(s, (s + steps) % count) for s in range(count)])  25.2 us
    ppermute x10, starting transfers between devices, moved(): lax.ppermute(value, 'dp', [(s, (s + steps) % count) for s in range(count)])  15.5 us
    all_to_all x1, starting transfers between devices, on_device(): lax.all_to_all(back.reshape(experts, 2 * width, features), 'expert', spli...  15.3 us
    all_to_all x1, starting transfers between devices, on_device(): lax.all_to_all(send.reshape(experts, 2 * width, features), 'expert', spli...  13.1 us
    all_to_all x1, waiting for transfers between devices, on_device(): lax.all_to_all(back.reshape(experts, 2 * width, features), 'expert', spli...  6.63 us
  transfers between devices with their start and end apart: 12, of which 9 were waited for; matrix products, arithmetic and copies ran while one was open for 2% of the time, Pallas kernels for 19%

profile of v2, /device:TPU:1, one launch (start us, length us, event | category | flops | bytes accessed | tf_op | source)
XLA Modules:
  0.0 136.8 jit_solution(1793420781346730787)
XLA Ops:
  0.6 2.1 %collective-permute-start = (bf16[1440,360]{1,0:T(8,128)(2,1)}, bf16[1440,360]{1,0:T(8,128)(2,1)}, u32[]{:S(2)}, u32[]{:S(2)}) collective-permute-start(bf16[1440,360]{1,0:T(8,128)(2,1)} %bitcast.16), channel_id=1, source_target_pairs={{0,1},{1,2},{2,3},{3,0},{4,5},{5,6},{6,7},{7,4},{8,9},{9,10},{10,1... | collective-permute-start | bytes 3110408 | tf_op jit(solution)/shard_map/ppermute | solution.py:15
  2.7 1.4 collective-permute-start.1
  4.8 3.5 %shard_map.112 = bf16[512,1440]{1,0:T(8,128)(2,1)} custom-call(s32[1]{0:T(128)S(6)} %copy.12.count_ref, s32[8]{0:T(128)} %plan_hbm.3, s32[4,128]{1,0:T(4,128)} %bitcast.27, s32[4,128]{1,0:T(4,128)} %bitcast.29, bf16[1440,128]{1,0:T(8,128)(2,1)} %bitcast.25, bf16[1440,128]{1,0:T(8,128)(2,1)} %bitcast.26), custom_call_target="tpu_custom_call" | custom-call | flops 566231040 | bytes 2215972 | tf_op jit(solution)/shard_map/pallas_call | solution.py:44
  8.3 13.1 %all-to-all-start = ((bf16[64,8,1440]{2,1,0:T(8,128)(2,1)}), bf16[64,8,1440]{2,1,0:T(8,128)(2,1)S(1)}, u32[]{:S(2)}, u32[]{:S(2)}) async-start(bf16[64,8,1440]{2,1,0:T(8,128)(2,1)} %bitcast.6), calls=%async_computation | async-start | bytes 3145728 | tf_op jit(solution)/shard_map/all_to_all | solution.py:357
  21.5 2.7 %collective-permute-start.3 = (bf16[1440,360]{1,0:T(8,128)(2,1)S(1)}, bf16[1440,360]{1,0:T(8,128)(2,1)}, u32[]{:S(2)}, u32[]{:S(2)}) collective-permute-start(bf16[1440,360]{1,0:T(8,128)(2,1)S(1)} %bitcast.18), channel_id=1, source_target_pairs={{0,3},{1,0},{2,1},{3,2},{4,7},{5,4},{6,5},{7,6},{8,11},{9,8},{10,9... | collective-permute-start | bytes 3110408 | tf_op jit(solution)/shard_map/ppermute | solution.py:15
  24.2 2.0 %collective-permute-done.refs_2_ = bf16[1440,360]{1,0:T(8,128)(2,1)} collective-permute-done((bf16[1440,360]{1,0:T(8,128)(2,1)}, bf16[1440,360]{1,0:T(8,128)(2,1)}, u32[]{:S(2)}, u32[]{:S(2)}) %collective-permute-start) | collective-permute-done | bytes 1036832 | tf_op jit(solution)/shard_map/ppermute | solution.py:15
  26.2 1.5 %collective-permute-done.1.refs_5_ = bf16[360,1440]{1,0:T(8,128)(2,1)} collective-permute-done((bf16[360,1440]{1,0:T(8,128)(2,1)}, bf16[360,1440]{1,0:T(8,128)(2,1)}, u32[]{:S(2)}, u32[]{:S(2)}) %collective-permute-start.1) | collective-permute-done | bytes 1036832 | tf_op jit(solution)/shard_map/ppermute | solution.py:15
  27.7 1.6 %collective-permute-start.4 = (bf16[1440,360]{1,0:T(8,128)(2,1)}, bf16[1440,360]{1,0:T(8,128)(2,1)}, u32[]{:S(2)}, u32[]{:S(2)}) collective-permute-start(bf16[1440,360]{1,0:T(8,128)(2,1)} %collective-permute-done.refs_2_), channel_id=1, source_target_pairs={{0,1},{1,2},{2,3},{3,0},{4,5},{5,6},{6,7},{7,4},{8,9},{9,10},{10,1... | collective-permute-start | bytes 3110408 | tf_op jit(solution)/shard_map/ppermute | solution.py:15
  32.6 28.6 %all-to-all-done = bf16[64,8,1440]{2,1,0:T(8,128)(2,1)S(1)} async-done(((bf16[64,8,1440]{2,1,0:T(8,128)(2,1)}), bf16[64,8,1440]{2,1,0:T(8,128)(2,1)S(1)}, u32[]{:S(2)}, u32[]{:S(2)}) %all-to-all-start) | async-done | bytes 1474592 | tf_op jit(solution)/shard_map/all_to_all | solution.py:357
  61.2 7.2 %shard_map.113 = (bf16[256,1440]{1,0:T(8,128)(2,1)S(1)}, bf16[256,1440]{1,0:T(8,128)(2,1)S(1)}, f32[256,1440]{1,0:T(8,128)S(1)}, f32[256,1440]{1,0:T(8,128)S(1)}) custom-call(bf16[512,1440]{1,0:T(8,128)(2,1)S(1)} %bitcast.15, bf16[1440,360]{1,0:T(8,128)(2,1)} %bitcast.17, bf16[360,1440]{1,0:T(8,128)(2,1)} %bitcast.22, ...), custom_call_target="tpu_custom_call" | custom-call | flops 3940024320 | bytes 12119040 | tf_op jit(solution)/shard_map/pallas_call | solution.py:44
  69.0 2.7 %collective-permute-start.8 = (bf16[1440,512]{1,0:T(8,128)(2,1)S(1)}, bf16[1440,512]{1,0:T(8,128)(2,1)}, u32[]{:S(2)}, u32[]{:S(2)}) collective-permute-start(bf16[1440,512]{1,0:T(8,128)(2,1)S(1)} %shard_map.116.refs_0_), channel_id=1, source_target_pairs={{0,3},{1,0},{2,1},{3,2},{4,7},{5,4},{6,5},{7,6},{8,11},{9,8},{10,9... | collective-permute-start | bytes 4423688 | tf_op jit(solution)/shard_map/ppermute | solution.py:15
  71.6 1.9 %collective-permute-done.4.wi_hbm = bf16[1440,360]{1,0:T(8,128)(2,1)} collective-permute-done((bf16[1440,360]{1,0:T(8,128)(2,1)}, bf16[1440,360]{1,0:T(8,128)(2,1)}, u32[]{:S(2)}, u32[]{:S(2)}) %collective-permute-start.4) | collective-permute-done | bytes 1036832 | tf_op jit(solution)/shard_map/ppermute | solution.py:15
  73.6 1.5 %collective-permute-done.5.wo_hbm = bf16[360,1440]{1,0:T(8,128)(2,1)} collective-permute-done((bf16[360,1440]{1,0:T(8,128)(2,1)}, bf16[360,1440]{1,0:T(8,128)(2,1)}, u32[]{:S(2)}, u32[]{:S(2)}) %collective-permute-start.5) | collective-permute-done | bytes 1036832 | tf_op jit(solution)/shard_map/ppermute | solution.py:15
  75.1 4.9 %shard_map.114 = bf16[512,1440]{1,0:T(8,128)(2,1)} custom-call(bf16[256,1440]{1,0:T(8,128)(2,1)S(1)} %get-tuple-element.27.x_ref, bf16[256,1440]{1,0:T(8,128)(2,1)S(1)} %get-tuple-element.28.y_ref, bf16[1440,360]{1,0:T(8,128)(2,1)} %collective-permute-done.4.wi_hbm, bf16[360,1440]{1,0:T(8,128)(2,1)} %collective-permute-done.5.wo_hbm, ...), custom_call_target="tpu_custom_call" | custom-call | flops 1816657920 | bytes 7971840 | tf_op jit(solution)/shard_map/pallas_call | solution.py:44
  79.9 15.3 %all-to-all-start.1 = ((bf16[64,8,1440]{2,1,0:T(8,128)(2,1)}), bf16[64,8,1440]{2,1,0:T(8,128)(2,1)S(1)}, u32[]{:S(2)}, u32[]{:S(2)}) async-start(bf16[64,8,1440]{2,1,0:T(8,128)(2,1)} %bitcast.8), calls=%async_computation.1 | async-start | bytes 3145728 | tf_op jit(solution)/shard_map/all_to_all | solution.py:416
  95.3 9.8 %collective-permute-done.6.refs_1_ = bf16[1440,512]{1,0:T(8,128)(2,1)} collective-permute-done((bf16[1440,512]{1,0:T(8,128)(2,1)S(1)}, bf16[1440,512]{1,0:T(8,128)(2,1)}, u32[]{:S(2)}, u32[]{:S(2)}) %collective-permute-start.6) | collective-permute-done | bytes 1474592 | tf_op jit(solution)/shard_map/ppermute | solution.py:15
  106.3 2.2 %collective-permute-start.7 = (bf16[1440,256]{1,0:T(8,128)(2,1)S(1)}, bf16[1440,256]{1,0:T(8,128)(2,1)S(1)}, u32[]{:S(2)}, u32[]{:S(2)}) collective-permute-start(bf16[1440,256]{1,0:T(8,128)(2,1)S(1)} %slice.8), channel_id=1, source_target_pairs={{0,1},{1,2},{2,3},{3,0},{4,5},{5,6},{6,7},{7,4},{8,9},{9,10},{10,1... | collective-permute-start | bytes 2211848 | tf_op jit(solution)/shard_map/ppermute | solution.py:15
  109.7 1.7 %collective-permute-start.9 = (bf16[1440,256]{1,0:T(8,128)(2,1)S(1)}, bf16[1440,256]{1,0:T(8,128)(2,1)S(1)}, u32[]{:S(2)}, u32[]{:S(2)}) collective-permute-start(bf16[1440,256]{1,0:T(8,128)(2,1)S(1)} %slice.9), channel_id=1, source_target_pairs={{0,3},{1,0},{2,1},{3,2},{4,7},{5,4},{6,5},{7,6},{8,11},{9,8},{10,9... | collective-permute-start | bytes 2211848 | tf_op jit(solution)/shard_map/ppermute | solution.py:15
  111.3 5.9 %shard_map.117 = (f32[360,1440]{1,0:T(8,128)S(1)}, f32[360,1440]{1,0:T(8,128)S(1)}) custom-call(bf16[360,1440]{1,0:T(8,128)(2,1)S(1)} %copy-done.3, bf16[360,1440]{1,0:T(8,128)(2,1)S(1)} %bitcast.23, bf16[1440,512]{1,0:T(8,128)(2,1)S(1)} %shard_map.116.refs_0_, bf16[1440,512]{1,0:T(8,128)(2,1)} %collective-permute-done.6.refs_1_, ...), custom_call_target="tpu_custom_call" | custom-call | flops 2123366400 | bytes 10644480 | tf_op jit(solution)/shard_map/pallas_call | solution.py:44
  117.2 6.6 %collective-permute-done.7.x_ref = bf16[1440,256]{1,0:T(8,128)(2,1)S(1)} collective-permute-done((bf16[1440,256]{1,0:T(8,128)(2,1)S(1)}, bf16[1440,256]{1,0:T(8,128)(2,1)S(1)}, u32[]{:S(2)}, u32[]{:S(2)}) %collective-permute-start.7) | collective-permute-done | bytes 737312 | tf_op jit(solution)/shard_map/ppermute | solution.py:15
  123.8 1.9 %collective-permute-done.9.y_ref = bf16[1440,256]{1,0:T(8,128)(2,1)S(1)} collective-permute-done((bf16[1440,256]{1,0:T(8,128)(2,1)S(1)}, bf16[1440,256]{1,0:T(8,128)(2,1)S(1)}, u32[]{:S(2)}, u32[]{:S(2)}) %collective-permute-start.9) | collective-permute-done | bytes 737312 | tf_op jit(solution)/shard_map/ppermute | solution.py:15
  125.7 2.8 %shard_map.118 = (bf16[1440,360]{1,0:T(8,128)(2,1)}, bf16[360,1440]{1,0:T(8,128)(2,1)}) custom-call(bf16[360,1440]{1,0:T(8,128)(2,1)S(1)} %copy-done.3, bf16[360,1440]{1,0:T(8,128)(2,1)S(1)} %bitcast.24, bf16[1440,256]{1,0:T(8,128)(2,1)S(1)} %collective-permute-done.7.x_ref, bf16[1440,256]{1,0:T(8,128)(2,1)S(1)} %collective-permute-done.9.y_ref, ...), custom_call_target="tpu_custom_call" | custom-call | flops 13271040000 | bytes 9768960 | tf_op jit(solution)/shard_map/pallas_call | solution.py:44
  128.5 6.6 %all-to-all-done.1 = bf16[64,8,1440]{2,1,0:T(8,128)(2,1)S(1)} async-done(((bf16[64,8,1440]{2,1,0:T(8,128)(2,1)}), bf16[64,8,1440]{2,1,0:T(8,128)(2,1)S(1)}, u32[]{:S(2)}, u32[]{:S(2)}) %all-to-all-start.1) | async-done | bytes 1474592 | tf_op jit(solution)/shard_map/all_to_all | solution.py:416
  135.1 1.7 %shard_map.115 = (bf16[1440,128]{1,0:T(8,128)(2,1)}, bf16[1440,128]{1,0:T(8,128)(2,1)}) custom-call(bf16[384,512]{1,0:T(8,128)(2,1)S(1)} %get-tuple-element.22.get_ref, bf16[512,1440]{1,0:T(8,128)(2,1)S(1)} %bitcast.14), custom_call_target="tpu_custom_call" | custom-call | flops 566231040 | bytes 2605056 | tf_op jit(solution)/shard_map/pallas_call | solution.py:44
  (18 shorter events, 6.3 us)
Async XLA Ops:
  0.6 25.5 %collective-permute-start = (bf16[1440,360]{1,0:T(8,128)(2,1)}, bf16[1440,360]{1,0:T(8,128)(2,1)}, u32[]{:S(2)}, u32[]{:S(2)}) collective-permute-start(bf16[1440,360]{1,0:T(8,128)(2,1)} %bitcast.16), channel_id=1, source_target_pairs={{0,1},{1,2},{2,3},{3,0},{4,5},{5,6},{6,7},{7,4},{8,9},{9,10},{10,1... | collective-permute-start | bytes 3110408 | tf_op jit(solution)/shard_map/ppermute | solution.py:15
  2.7 24.9 %collective-permute-start.1 = (bf16[360,1440]{1,0:T(8,128)(2,1)}, bf16[360,1440]{1,0:T(8,128)(2,1)}, u32[]{:S(2)}, u32[]{:S(2)}) collective-permute-start(bf16[360,1440]{1,0:T(8,128)(2,1)} %bitcast.20), channel_id=1, source_target_pairs={{0,3},{1,0},{2,1},{3,2},{4,7},{5,4},{6,5},{7,6},{8,11},{9,8},{10,9... | collective-permute-start | bytes 3110408 | tf_op jit(solution)/shard_map/ppermute | solution.py:15
  8.3 13.2 %copy-start = (bf16[1,1440,360]{2,1,0:T(8,128)(2,1)S(1)}, bf16[1,1440,360]{2,1,0:T(8,128)(2,1)}, u32[]{:S(2)}) copy-start(bf16[1,1440,360]{2,1,0:T(8,128)(2,1)} %param.13) | copy-start | bytes 3110404
  8.3 52.9 %all-to-all-start = ((bf16[64,8,1440]{2,1,0:T(8,128)(2,1)}), bf16[64,8,1440]{2,1,0:T(8,128)(2,1)S(1)}, u32[]{:S(2)}, u32[]{:S(2)}) async-start(bf16[64,8,1440]{2,1,0:T(8,128)(2,1)} %bitcast.6), calls=%async_computation | async-start | bytes 3145728 | tf_op jit(solution)/shard_map/all_to_all | solution.py:357
  21.4 39.8 %collective-permute-start.2 = (bf16[360,1440]{1,0:T(8,128)(2,1)}, bf16[360,1440]{1,0:T(8,128)(2,1)}, u32[]{:S(2)}, u32[]{:S(2)}) collective-permute-start(bf16[360,1440]{1,0:T(8,128)(2,1)} %bitcast.21), channel_id=1, source_target_pairs={{0,1},{1,2},{2,3},{3,0},{4,5},{5,6},{6,7},{7,4},{8,9},{9,10},{10,1... | collective-permute-start | bytes 3110408 | tf_op jit(solution)/shard_map/ppermute | solution.py:15
  21.5 39.7 %collective-permute-start.3 = (bf16[1440,360]{1,0:T(8,128)(2,1)S(1)}, bf16[1440,360]{1,0:T(8,128)(2,1)}, u32[]{:S(2)}, u32[]{:S(2)}) collective-permute-start(bf16[1440,360]{1,0:T(8,128)(2,1)S(1)} %bitcast.18), channel_id=1, source_target_pairs={{0,3},{1,0},{2,1},{3,2},{4,7},{5,4},{6,5},{7,6},{8,11},{9,8},{10,9... | collective-permute-start | bytes 3110408 | tf_op jit(solution)/shard_map/ppermute | solution.py:15
  27.7 45.9 %collective-permute-start.4 = (bf16[1440,360]{1,0:T(8,128)(2,1)}, bf16[1440,360]{1,0:T(8,128)(2,1)}, u32[]{:S(2)}, u32[]{:S(2)}) collective-permute-start(bf16[1440,360]{1,0:T(8,128)(2,1)} %collective-permute-done.refs_2_), channel_id=1, source_target_pairs={{0,1},{1,2},{2,3},{3,0},{4,5},{5,6},{6,7},{7,4},{8,9},{9,10},{10,1... | collective-permute-start | bytes 3110408 | tf_op jit(solution)/shard_map/ppermute | solution.py:15
  29.2 45.8 %collective-permute-start.5 = (bf16[360,1440]{1,0:T(8,128)(2,1)}, bf16[360,1440]{1,0:T(8,128)(2,1)}, u32[]{:S(2)}, u32[]{:S(2)}) collective-permute-start(bf16[360,1440]{1,0:T(8,128)(2,1)} %collective-permute-done.1.refs_5_), channel_id=1, source_target_pairs={{0,3},{1,0},{2,1},{3,2},{4,7},{5,4},{6,5},{7,6},{8,11},{9,8},{10,9... | collective-permute-start | bytes 3110408 | tf_op jit(solution)/shard_map/ppermute | solution.py:15
  31.6 1.0 copy-start.2
  68.9 36.3 %collective-permute-start.6 = (bf16[1440,512]{1,0:T(8,128)(2,1)S(1)}, bf16[1440,512]{1,0:T(8,128)(2,1)}, u32[]{:S(2)}, u32[]{:S(2)}) collective-permute-start(bf16[1440,512]{1,0:T(8,128)(2,1)S(1)} %shard_map.116.refs_0_), channel_id=1, source_target_pairs={{0,1},{1,2},{2,3},{3,0},{4,5},{5,6},{6,7},{7,4},{8,9},{9,10},{10,1... | collective-permute-start | bytes 4423688 | tf_op jit(solution)/shard_map/ppermute | solution.py:15
  69.0 39.5 %collective-permute-start.8 = (bf16[1440,512]{1,0:T(8,128)(2,1)S(1)}, bf16[1440,512]{1,0:T(8,128)(2,1)}, u32[]{:S(2)}, u32[]{:S(2)}) collective-permute-start(bf16[1440,512]{1,0:T(8,128)(2,1)S(1)} %shard_map.116.refs_0_), channel_id=1, source_target_pairs={{0,3},{1,0},{2,1},{3,2},{4,7},{5,4},{6,5},{7,6},{8,11},{9,8},{10,9... | collective-permute-start | bytes 4423688 | tf_op jit(solution)/shard_map/ppermute | solution.py:15
  79.9 55.1 %all-to-all-start.1 = ((bf16[64,8,1440]{2,1,0:T(8,128)(2,1)}), bf16[64,8,1440]{2,1,0:T(8,128)(2,1)S(1)}, u32[]{:S(2)}, u32[]{:S(2)}) async-start(bf16[64,8,1440]{2,1,0:T(8,128)(2,1)} %bitcast.8), calls=%async_computation.1 | async-start | bytes 3145728 | tf_op jit(solution)/shard_map/all_to_all | solution.py:416
  95.3 16.0 %copy-start.1 = (bf16[1,360,1440]{2,1,0:T(8,128)(2,1)S(1)}, bf16[1,360,1440]{2,1,0:T(8,128)(2,1)}, u32[]{:S(2)}) copy-start(bf16[1,360,1440]{2,1,0:T(8,128)(2,1)} %param.14) | copy-start | bytes 3110404
  95.3 16.0 %copy-start.3 = (bf16[360,1440]{1,0:T(8,128)(2,1)S(1)}, bf16[360,1440]{1,0:T(8,128)(2,1)}, u32[]{:S(2)}) copy-start(bf16[360,1440]{1,0:T(8,128)(2,1)} %copy-done.2) | copy-start | bytes 3110404
  106.3 17.5 %collective-permute-start.7 = (bf16[1440,256]{1,0:T(8,128)(2,1)S(1)}, bf16[1440,256]{1,0:T(8,128)(2,1)S(1)}, u32[]{:S(2)}, u32[]{:S(2)}) collective-permute-start(bf16[1440,256]{1,0:T(8,128)(2,1)S(1)} %slice.8), channel_id=1, source_target_pairs={{0,1},{1,2},{2,3},{3,0},{4,5},{5,6},{6,7},{7,4},{8,9},{9,10},{10,1... | collective-permute-start | bytes 2211848 | tf_op jit(solution)/shard_map/ppermute | solution.py:15
  109.7 16.0 %collective-permute-start.9 = (bf16[1440,256]{1,0:T(8,128)(2,1)S(1)}, bf16[1440,256]{1,0:T(8,128)(2,1)S(1)}, u32[]{:S(2)}, u32[]{:S(2)}) collective-permute-start(bf16[1440,256]{1,0:T(8,128)(2,1)S(1)} %slice.9), channel_id=1, source_target_pairs={{0,3},{1,0},{2,1},{3,2},{4,7},{5,4},{6,5},{7,6},{8,11},{9,8},{10,9... | collective-permute-start | bytes 2211848 | tf_op jit(solution)/shard_map/ppermute | solution.py:15
